TPU v7x, 256 devices: a whole 4x4x8 slice. The times are simulated.
256 devices in a mesh: band: 32 (over y, x, core), slab: 8 (over z).
Axes of the slice: x: 4, y: 4, z: 8, core: 2. Of those that a mesh axis runs over, the one named last changes fastest.
Arguments:
- orbitals: float32 [32, 128, 128, 128], P('band', 'slab'), may hold values from -6 to 6
- column_ids: int32 [8, 768], P('slab'), may hold values from 0 to 4095, as said below
- source_ids: int32 [2], replicated, may hold values from 0 to 31
Outputs:
- exchange: float32 [32, 128, 128, 128], P('band', 'slab')
- energy: float32 [32, 6144], P('band', 'slab')
Inputs may be any that keep to these rules, and one draw needn't show every extreme that they name: `column_ids`: A column is numbered c = (ky + 32) * 64 + kz + 32. Every column with ky^2 + kz^2 < 32^2 appears exactly once in the whole table; every other slot holds 0, a column outside that disk. One row holds 768 such disk columns.
All inputs are finite; a program needn't handle non-finite values.
Results may differ from a plain program's by a relative error of at most 0.0001.
Values sent between devices are 32-bit elements; how exact they have to be, the bound alone decides.
No kernel may reach another device: no remote copies, remote signals or barrier semaphores. Data moves between devices by JAX's collectives and lax.ppermute only.
A program may use at most 128 MiB of HBM per device.

v0:
```python
import math

import jax
import jax.numpy as jnp
import numpy as np
from jax import lax
from jax.experimental import pallas as pl
from jax.experimental.pallas import tpu as pltpu
from jax.sharding import PartitionSpec as P

G = 128
KCUT = 32
SLABS = 8
PLANES = 16
SLOTS = 768
ROWS = 8
LANES = 128


def split_table(table):
    high = table.astype(jnp.bfloat16)
    low = (table - high.astype(np.float64)).astype(jnp.bfloat16)
    return high, low


def waves(points):
    phase = np.arange(KCUT)[:, None] * np.arange(points)[None, :] % points
    angle = phase * (2.0 * math.pi / points)
    return np.cos(angle), np.sin(angle)


def basis_tables():
    cosine, sine = waves(G)
    along_x = np.concatenate([cosine, sine], axis=0)
    group_rows = []
    for slab in range(SLABS):
        group_rows.append(cosine[4 * slab : 4 * slab + 4])
        group_rows.append(sine[4 * slab : 4 * slab + 4])
    along_y = np.concatenate(group_rows, axis=0)
    along_z = np.zeros((2 * G, LANES))
    along_z[:G, :64] = along_x.T
    along_z[G:, 64:] = along_x.T
    return along_x, along_y, along_z


def bf16_parts(value):
    high = value.astype(jnp.bfloat16)
    low = (value - high.astype(jnp.float32)).astype(jnp.bfloat16)
    return high, low


def dot(a, b):
    return jnp.dot(a, b, preferred_element_type=jnp.float32)


def left_product(stacked, value):
    high, low = bf16_parts(value)
    rows = stacked.shape[0] // 2
    first = dot(stacked, high)
    return first[:rows] + first[rows:] + dot(stacked[:rows], low)


def wide_product(joined, value):
    high, low = bf16_parts(value)
    table = jnp.concatenate([joined, joined[:, :64]], axis=1)
    return dot(table, jnp.concatenate([high, high, low], axis=0))


def forward_kernel(place_ref, orbital_ref, ty_ref, tz_ref, *refs):
    piece_refs, out_refs = refs[:-SLABS], refs[-SLABS:]
    for p, piece_ref in enumerate(piece_refs):
        plane = place_ref[p] * 2
        orbital = orbital_ref[0, pl.ds(plane, 2)]
        pair0 = (piece_ref[0] * orbital).reshape(2 * G, G)
        pair1 = (piece_ref[1] * orbital).reshape(2 * G, G)
        high, low = bf16_parts(jnp.concatenate([pair0, pair1], axis=1))
        first = dot(high, tz_ref[...])
        along_z = first[:, :LANES] + first[:, LANES:] + dot(low, tz_ref[:, :LANES])
        for q in range(2):
            box = left_product(ty_ref[...], along_z[q * G : (q + 1) * G])
            for k in range(SLABS):
                out_refs[k][plane + q] = box[k * ROWS : (k + 1) * ROWS]


def filter_kernel(slab_ref, tx_ref, txt_ref, *refs):
    cols_refs, out_refs = refs[:SLABS], refs[SLABS:]

    def columns(j):
        return jnp.concatenate([ref[:, j, :] for ref in cols_refs], axis=0)

    lane = lax.broadcasted_iota(jnp.int32, (2 * KCUT, LANES), 1)
    row = lax.broadcasted_iota(jnp.int32, (2 * KCUT, LANES), 0)
    wave_z = lane % KCUT
    wave_x = row % KCUT
    scale = float(G) ** -3
    many_x = jnp.where(wave_x == 0, 1.0, 2.0)
    many_z = jnp.where(wave_z == 0, 1.0, 2.0)
    power_rows = []
    for j in range(4):
        wave_y = slab_ref[0] * 4 + j
        radius = wave_x * wave_x + wave_z * wave_z + wave_y * wave_y
        weight = jnp.where(
            radius < KCUT * KCUT, (4.0 * scale) / (1.0 + radius.astype(jnp.float32) / 1024.0), 0.0
        )
        weight = weight * many_x
        many_y = jnp.where(wave_y == 0, 1.0, 2.0)
        spread = weight * (many_z * many_y)
        cos_y = left_product(tx_ref[...], columns(j))
        sin_y = left_product(tx_ref[...], columns(j + 4))
        squares = jnp.sum(weight * (cos_y * cos_y + sin_y * sin_y), axis=0, keepdims=True)
        cross = cos_y * pltpu.roll(sin_y, 96, 1) - sin_y * pltpu.roll(cos_y, 96, 1)
        cross = 2.0 * jnp.sum(weight * cross, axis=0, keepdims=True)
        squares = squares + pltpu.roll(squares, 96, 1)
        same = squares - cross
        other = squares + cross
        same = same + pltpu.roll(same, 64, 1)
        other = other + pltpu.roll(other, 64, 1)
        first = lax.broadcasted_iota(jnp.int32, (1, LANES), 1) < KCUT
        power_rows.append(jnp.where(first, same, pltpu.roll(other, 32, 1)) * (1.0 / 64.0))
        for k, value in ((j, cos_y), (j + 4, sin_y)):
            back = wide_product(txt_ref[...], spread * value)
            for d in range(SLABS):
                out_refs[d][0:PLANES, k, :] = back[d * PLANES : (d + 1) * PLANES]
    power = jnp.concatenate(power_rows + power_rows, axis=0)
    for d in range(SLABS):
        out_refs[d][PLANES] = power


def inverse_kernel(place_ref, slab_ref, ids_ref, ty_ref, tz_ref, *refs):
    back_refs, piece_refs, exchange_ref, energy_ref = refs[:SLABS], refs[SLABS:-2], refs[-2], refs[-1]
    for p, piece_ref in enumerate(piece_refs):
        plane = place_ref[p] * 2
        rows = []
        for q in range(2):
            box = jnp.concatenate([ref[plane + q] for ref in back_refs], axis=0)
            rows.append(wide_product(ty_ref[...], box))
        high, low = bf16_parts(jnp.concatenate(rows, axis=0))
        pots = dot(high, tz_ref[0]) + dot(low, tz_ref[0]) + dot(high, tz_ref[1])
        value = piece_ref[0].reshape(2 * G, G) * pots[:, :G] + piece_ref[1].reshape(2 * G, G) * pots[:, G:]
        exchange_ref[0, pl.ds(plane, 2)] = value.reshape(2, G, G)
    power = jnp.concatenate([ref[PLANES] for ref in back_refs], axis=0)
    ids = ids_ref[...]
    wave_y = ids // 64 - KCUT
    wave_z = ids % 64 - KCUT
    size_y = jnp.abs(wave_y)
    size_z = jnp.abs(wave_z)
    group = (size_y // 4 + SLABS - slab_ref[0]) % SLABS
    row = jnp.where(size_y < KCUT, group * ROWS + size_y % 4, -1)
    pick = jnp.where(wave_y * wave_z < 0, size_z + KCUT, size_z)
    pick = jnp.where(size_z < KCUT, pick, -1)
    hot = (lax.broadcasted_iota(jnp.int32, (SLABS * ROWS, SLOTS), 0) == row).astype(jnp.bfloat16)
    transposed = power.T
    high, low = bf16_parts(transposed)
    rest = (transposed - high.astype(jnp.float32) - low.astype(jnp.float32)).astype(jnp.bfloat16)
    table = dot(high, hot) + dot(low, hot) + dot(rest, hot)
    lane = lax.broadcasted_iota(jnp.int32, (LANES, SLOTS), 0)
    energy_ref[...] = jnp.sum(jnp.where(lane == pick, table, 0.0), axis=0, keepdims=True)


VMEM = pl.BlockSpec(memory_space=pltpu.VMEM)
SMEM = pl.BlockSpec(memory_space=pltpu.SMEM)


def band_index(y, x, core):
    return (y * 4 + x) * 2 + core


def gray(place):
    return place ^ (place >> 1)


PLACE_OF_CODE = [0, 1, 3, 2]


def neighbour(y, x, dim):
    code = gray(x) | (gray(y) << 2)
    code = code ^ (1 << dim)
    return PLACE_OF_CODE[code >> 2], PLACE_OF_CODE[code & 3]


def cube_pairs(slot, step):
    pairs = []
    for y in range(4):
        for x in range(4):
            for core in range(2):
                there = neighbour(y, x, (2 * core + slot + step) % 4)
                pairs.append((band_index(y, x, core), band_index(*there, core)))
    return pairs


CORE_PAIRS = [(i, i ^ 1) for i in range(32)]


def bit(code, position):
    return (code >> position) & 1


def broadcast_sources(orbitals, source_ids):
    me = lax.axis_index("band")
    core = me % 2
    x = (me // 2) % 4
    y = me // 8
    code = gray(x) | (gray(y) << 2)
    orbital = orbitals[0].reshape(2, 2, 2, 2, G, G)
    mine = lax.dynamic_index_in_dim(orbital, core, 0, keepdims=False)
    theirs = lax.ppermute(
        lax.dynamic_index_in_dim(orbital, 1 - core, 0, keepdims=False), "band", CORE_PAIRS
    )
    source_x = (source_ids // 2) % 4
    source_y = source_ids // 8
    relative = code ^ (gray(source_x) | (gray(source_y) << 2))
    is_mine = (source_ids % 2 == core)[:, None, None, None]

    def choose(slot, step):
        return jnp.where(flags[slot][step - 1], gots[slot], keeps[slot])

    places, partner_places, sides = [], [], []
    for slot in range(2):
        side = bit(code, (2 * core + slot) % 4)
        sides.append(side)
        partner_side = bit(code, (2 * (1 - core) + slot) % 4)
        places.append((4 * core + 2 * slot + side, 4 * core + 2 * slot + 1 - side))
        base = 4 * (1 - core) + 2 * slot
        partner_places.append((base + partner_side, base + 1 - partner_side))

    def half(slot, which):
        own = lax.dynamic_index_in_dim(mine[slot], which, 0, keepdims=False)
        other = lax.dynamic_index_in_dim(theirs[slot], which, 0, keepdims=False)
        return jnp.where(is_mine, own[None], other[None])

    def send(slot, value, step, name):
        return lax.ppermute(value, "band", CORE_PAIRS if name == "swap" else cube_pairs(slot, step))

    away = lax.optimization_barrier([half(slot, 1 - sides[slot]) for slot in range(2)])
    gots = [send(slot, away[slot], 0, "send") for slot in range(2)]
    keeps = lax.optimization_barrier([half(slot, sides[slot]) for slot in range(2)])
    flags = [
        [relative != 0] + [bit(relative, (2 * core + slot + step) % 4) == 1 for step in range(1, 4)]
        for slot in range(2)
    ]
    flags = jax.tree.map(lambda flag: flag[:, None, None, None], flags)
    flags = lax.optimization_barrier(flags)
    for step in range(1, 4):
        for slot in range(2):
            keeps[slot] = choose(slot, step)
            gots[slot] = send(slot, keeps[slot], step, "send")
    swapped, swapped_gots = [], []
    for slot in range(2):
        keeps[slot] = choose(slot, 4)
        gots[slot] = send(slot, keeps[slot], 4, "send")
        swapped.append(send(slot, keeps[slot], 4, "swap"))
    for slot in range(2):
        swapped_gots.append(send(slot, gots[slot], 5, "swap"))
    pieces = keeps + swapped + gots + swapped_gots
    order = [p[0] for p in places] + [p[0] for p in partner_places]
    order += [p[1] for p in places] + [p[1] for p in partner_places]
    return pieces, jnp.stack(order).astype(jnp.int32)


def call(kernel, specs, shapes):
    single = isinstance(shapes, jax.ShapeDtypeStruct)
    return pl.pallas_call(
        kernel,
        out_shape=shapes,
        in_specs=specs,
        out_specs=VMEM if single else tuple(VMEM for _ in shapes),
        compiler_params=pltpu.CompilerParams(vmem_limit_bytes=32 << 20),
    )


def turned(table, block, axis, join):
    forms = [np.roll(table, -block * slab, axis=axis) for slab in range(SLABS)]
    return jnp.asarray(np.stack([np.concatenate(split_table(form), axis=join) for form in forms]))


def turn(tables, slab):
    return lax.dynamic_index_in_dim(tables, slab, 0, keepdims=False)


FAR_ORDER = (4, 3, 5, 2, 6, 1, 7)


def exchange_blocks(blocks):
    came = [blocks[0]] + [None] * (SLABS - 1)
    for k in FAR_ORDER:
        pairs = [(z, (z + k) % SLABS) for z in range(SLABS)]
        came[SLABS - k] = lax.ppermute(blocks[k], "slab", pairs)
    return came


def step(orbitals, column_ids, source_ids):
    along_x, along_y, along_z = basis_tables()
    forward_y = turned(along_y, ROWS, 0, 0)
    forward_z = jnp.asarray(np.concatenate(split_table(along_z), axis=1))
    forward_x = turned(along_x, PLANES, 1, 0)
    inverse_x = turned(along_x.T, PLANES, 0, 1)
    inverse_y = turned(along_y.T, ROWS, 1, 1)
    inverse_z = jnp.asarray(np.stack(split_table(along_z.T), axis=0))

    f32 = jnp.float32
    slab = lax.axis_index("slab").astype(jnp.int32)
    slab_ref = slab.reshape(1)
    pieces, places = broadcast_sources(orbitals, source_ids)
    block = jax.ShapeDtypeStruct((PLANES, ROWS, LANES), f32)
    columns = call(
        forward_kernel, [SMEM] + [VMEM] * (3 + len(pieces)), (block,) * SLABS
    )(places, orbitals, turn(forward_y, slab), forward_z, *pieces)
    columns = exchange_blocks(columns)
    block = jax.ShapeDtypeStruct((PLANES + 1, ROWS, LANES), f32)
    back = call(
        filter_kernel, [SMEM] + [VMEM] * (2 + SLABS), (block,) * SLABS
    )(slab_ref, turn(forward_x, slab), turn(inverse_x, slab), *columns)
    back = exchange_blocks(back)
    exchange, energy = call(
        inverse_kernel,
        [SMEM] * 2 + [VMEM] * (3 + SLABS + len(pieces)),
        (
            jax.ShapeDtypeStruct((1, PLANES, G, G), f32),
            jax.ShapeDtypeStruct((1, SLOTS), f32),
        ),
    )(places, slab_ref, column_ids, turn(inverse_y, slab), inverse_z, *back, *pieces)
    return exchange, energy


def solution(mesh):
    placed = (P("band", "slab", None, None), P("slab", None), P())
    return jax.shard_map(
        step,
        mesh=mesh,
        in_specs=placed,
        out_specs=(P("band", "slab", None, None), P("band", "slab")),
        check_vma=False,
    )
```

profile of v0, /device:TPU:1, one launch (start us, length us, event | category | flops | bytes accessed | tf_op | source)
XLA Modules:
  0.0 99.1 jit_solution(13458660784739602938)
XLA Ops:
  1.8 3.3 %collective-permute-start = (f32[2,2,2,128,128]{4,3,2,1,0:T(8,128)S(1)}, f32[2,2,2,128,128]{4,3,2,1,0:T(8,128)S(1)}, u32[]{:S(2)}, u32[]{:S(2)}) collective-permute-start(f32[2,2,2,128,128]{4,3,2,1,0:T(8,128)S(1)} %dynamic-slice_bitcast_fusion), channel_id=1, source_target_pairs={{0,8},{8,0},{16,24},{24,16},{32,40},{40,32},{48,56},{56,48},{64,72... | collective-permute-start | bytes 1572872 | tf_op jit(solution)/shard_map/ppermute | solution.py:206
  7.0 1.5 %collective-permute-start.5 = (f32[2,2,128,128]{3,2,1,0:T(8,128)S(1)}, f32[2,2,128,128]{3,2,1,0:T(8,128)S(1)}, u32[]{:S(2)}, u32[]{:S(2)}) collective-permute-start(f32[2,2,128,128]{3,2,1,0:T(8,128)S(1)} %get-tuple-element.40), channel_id=1, source_target_pairs={{0,48},{8,200},{16,32},{24,216},{32,16},{40,232},{48,0},{56,248},{... | collective-permute-start | bytes 786440 | tf_op jit(solution)/shard_map/ppermute | solution.py:232
  8.5 4.0 %collective-permute-done.1 = f32[2,2,128,128]{3,2,1,0:T(8,128)S(1)} collective-permute-done((f32[2,2,128,128]{3,2,1,0:T(8,128)S(1)}, f32[2,2,128,128]{3,2,1,0:T(8,128)S(1)}, u32[]{:S(2)}, u32[]{:S(2)}) %collective-permute-start.1) | collective-permute-done | bytes 262176 | tf_op jit(solution)/shard_map/ppermute | solution.py:232
  15.1 4.3 %collective-permute-done.2 = f32[2,2,128,128]{3,2,1,0:T(8,128)S(1)} collective-permute-done((f32[2,2,128,128]{3,2,1,0:T(8,128)S(1)}, f32[2,2,128,128]{3,2,1,0:T(8,128)S(1)}, u32[]{:S(2)}, u32[]{:S(2)}) %collective-permute-start.2) | collective-permute-done | bytes 262176 | tf_op jit(solution)/shard_map/ppermute | solution.py:232
  19.8 2.4 %collective-permute-start.7 = (f32[2,2,128,128]{3,2,1,0:T(8,128)S(1)}, f32[2,2,128,128]{3,2,1,0:T(8,128)S(1)}, u32[]{:S(2)}, u32[]{:S(2)}) collective-permute-start(f32[2,2,128,128]{3,2,1,0:T(8,128)S(1)} %broadcast_select_fusion.5), channel_id=1, source_target_pairs={{0,192},{8,56},{16,208},{24,40},{32,224},{40,24},{48,240},{56,8},{... | collective-permute-start | bytes 786440 | tf_op jit(solution)/shard_map/ppermute | solution.py:232
  22.1 3.0 %collective-permute-done.3 = f32[2,2,128,128]{3,2,1,0:T(8,128)S(1)} collective-permute-done((f32[2,2,128,128]{3,2,1,0:T(8,128)S(1)}, f32[2,2,128,128]{3,2,1,0:T(8,128)S(1)}, u32[]{:S(2)}, u32[]{:S(2)}) %collective-permute-start.3) | collective-permute-done | bytes 262176 | tf_op jit(solution)/shard_map/ppermute | solution.py:232
  26.8 5.0 %collective-permute-done.4 = f32[2,2,128,128]{3,2,1,0:T(8,128)S(1)} collective-permute-done((f32[2,2,128,128]{3,2,1,0:T(8,128)S(1)}, f32[2,2,128,128]{3,2,1,0:T(8,128)S(1)}, u32[]{:S(2)}, u32[]{:S(2)}) %collective-permute-start.4) | collective-permute-done | bytes 262176 | tf_op jit(solution)/shard_map/ppermute | solution.py:232
  32.1 2.6 %collective-permute-start.12 = (f32[2,2,128,128]{3,2,1,0:T(8,128)S(1)}, f32[2,2,128,128]{3,2,1,0:T(8,128)S(1)}, u32[]{:S(2)}, u32[]{:S(2)}) collective-permute-start(f32[2,2,128,128]{3,2,1,0:T(8,128)S(1)} %broadcast_select_fusion.7.refs_1_.refs_9_), channel_id=1, source_target_pairs={{0,48},{8,200},{16,32},{24,216},{32,16},{40,232},{48,0},{56,248},{... | collective-permute-start | bytes 786440 | tf_op jit(solution)/shard_map/ppermute | solution.py:232
  34.7 4.4 %collective-permute-start.9 = (f32[2,2,128,128]{3,2,1,0:T(8,128)S(1)}, f32[2,2,128,128]{3,2,1,0:T(8,128)S(1)}, u32[]{:S(2)}, u32[]{:S(2)}) collective-permute-start(f32[2,2,128,128]{3,2,1,0:T(8,128)S(1)} %broadcast_select_fusion.11.refs_0_.refs_8_), channel_id=1, source_target_pairs={{0,8},{8,0},{16,24},{24,16},{32,40},{40,32},{48,56},{56,48},{64,72... | collective-permute-start | bytes 786440 | tf_op jit(solution)/shard_map/ppermute | solution.py:232
  39.1 3.3 %collective-permute-start.13 = (f32[2,2,128,128]{3,2,1,0:T(8,128)S(1)}, f32[2,2,128,128]{3,2,1,0:T(8,128)S(1)}, u32[]{:S(2)}, u32[]{:S(2)}) collective-permute-start(f32[2,2,128,128]{3,2,1,0:T(8,128)S(1)} %collective-permute-done.11.refs_4_.refs_12_), channel_id=1, source_target_pairs={{0,8},{8,0},{16,24},{24,16},{32,40},{40,32},{48,56},{56,48},{64,72... | collective-permute-start | bytes 786440 | tf_op jit(solution)/shard_map/ppermute | solution.py:232
  42.4 1.5 %collective-permute-start.14 = (f32[2,2,128,128]{3,2,1,0:T(8,128)S(1)}, f32[2,2,128,128]{3,2,1,0:T(8,128)S(1)}, u32[]{:S(2)}, u32[]{:S(2)}) collective-permute-start(f32[2,2,128,128]{3,2,1,0:T(8,128)S(1)} %collective-permute-done.12.refs_5_.refs_13_), channel_id=1, source_target_pairs={{0,8},{8,0},{16,24},{24,16},{32,40},{40,32},{48,56},{56,48},{64,72... | collective-permute-start | bytes 786440 | tf_op jit(solution)/shard_map/ppermute | solution.py:232
  45.1 2.5 %shard_map.104 = (f32[16,8,128]{2,1,0:T(8,128)S(1)}, f32[16,8,128]{2,1,0:T(8,128)S(1)}, f32[16,8,128]{2,1,0:T(8,128)S(1)}, f32[16,8,128]{2,1,0:T(8,128)S(1)}, f3...) custom-call(s32[8]{0:T(128)S(1)} %stack.35.place_ref, ...), custom_call_target="tpu_custom_call" | custom-call | tf_op jit(solution)/shard_map/pallas_call | solution.py:305
  47.6 5.6 %collective-permute-start.15 = (f32[16,8,128]{2,1,0:T(8,128)S(1)}, f32[16,8,128]{2,1,0:T(8,128)S(1)}, u32[]{:S(2)}, u32[]{:S(2)}) collective-permute-start(f32[16,8,128]{2,1,0:T(8,128)S(1)} %get-tuple-element.43), channel_id=1, source_target_pairs={{0,7},{1,0},{2,1},{3,2},{4,3},{5,4},{6,5},{7,6},{8,15},{9,8},{10,9... | collective-permute-start | bytes 196616 | tf_op jit(solution)/shard_map/ppermute | solution.py:287
  54.8 4.5 %collective-permute-start.18 = (f32[16,8,128]{2,1,0:T(8,128)S(1)}, f32[16,8,128]{2,1,0:T(8,128)S(1)}, u32[]{:S(2)}, u32[]{:S(2)}) collective-permute-start(f32[16,8,128]{2,1,0:T(8,128)S(1)} %get-tuple-element.46), channel_id=1, source_target_pairs={{0,4},{1,5},{2,6},{3,7},{4,0},{5,1},{6,2},{7,3},{8,12},{9,13},{10,... | collective-permute-start | bytes 196616 | tf_op jit(solution)/shard_map/ppermute | solution.py:287
  59.3 2.2 %collective-permute-start.20 = (f32[16,8,128]{2,1,0:T(8,128)S(1)}, f32[16,8,128]{2,1,0:T(8,128)S(1)}, u32[]{:S(2)}, u32[]{:S(2)}) collective-permute-start(f32[16,8,128]{2,1,0:T(8,128)S(1)} %get-tuple-element.48), channel_id=1, source_target_pairs={{0,2},{1,3},{2,4},{3,5},{4,6},{5,7},{6,0},{7,1},{8,10},{9,11},{10,... | collective-permute-start | bytes 196616 | tf_op jit(solution)/shard_map/ppermute | solution.py:287
  61.5 1.4 %collective-permute-start.21 = (f32[16,8,128]{2,1,0:T(8,128)S(1)}, f32[16,8,128]{2,1,0:T(8,128)S(1)}, u32[]{:S(2)}, u32[]{:S(2)}) collective-permute-start(f32[16,8,128]{2,1,0:T(8,128)S(1)} %get-tuple-element.49), channel_id=1, source_target_pairs={{0,1},{1,2},{2,3},{3,4},{4,5},{5,6},{6,7},{7,0},{8,9},{9,10},{10,1... | collective-permute-start | bytes 196616 | tf_op jit(solution)/shard_map/ppermute | solution.py:287
  63.7 1.8 %collective-permute-done.19.refs_5_ = f32[16,8,128]{2,1,0:T(8,128)S(1)} collective-permute-done((f32[16,8,128]{2,1,0:T(8,128)S(1)}, f32[16,8,128]{2,1,0:T(8,128)S(1)}, u32[]{:S(2)}, u32[]{:S(2)}) %collective-permute-start.19) | collective-permute-done | bytes 65568 | tf_op jit(solution)/shard_map/ppermute | solution.py:287
  65.5 5.1 %collective-permute-done.20.refs_6_ = f32[16,8,128]{2,1,0:T(8,128)S(1)} collective-permute-done((f32[16,8,128]{2,1,0:T(8,128)S(1)}, f32[16,8,128]{2,1,0:T(8,128)S(1)}, u32[]{:S(2)}, u32[]{:S(2)}) %collective-permute-start.20) | collective-permute-done | bytes 65568 | tf_op jit(solution)/shard_map/ppermute | solution.py:287
  75.1 3.8 %collective-permute-start.24 = (f32[17,8,128]{2,1,0:T(8,128)S(1)}, f32[17,8,128]{2,1,0:T(8,128)S(1)}, u32[]{:S(2)}, u32[]{:S(2)}) collective-permute-start(f32[17,8,128]{2,1,0:T(8,128)S(1)} %get-tuple-element.53), channel_id=1, source_target_pairs={{0,5},{1,6},{2,7},{3,0},{4,1},{5,2},{6,3},{7,4},{8,13},{9,14},{10,... | collective-permute-start | bytes 208904 | tf_op jit(solution)/shard_map/ppermute | solution.py:287
  79.8 2.2 %collective-permute-start.26 = (f32[17,8,128]{2,1,0:T(8,128)S(1)}, f32[17,8,128]{2,1,0:T(8,128)S(1)}, u32[]{:S(2)}, u32[]{:S(2)}) collective-permute-start(f32[17,8,128]{2,1,0:T(8,128)S(1)} %get-tuple-element.55), channel_id=1, source_target_pairs={{0,3},{1,4},{2,5},{3,6},{4,7},{5,0},{6,1},{7,2},{8,11},{9,12},{10,... | collective-permute-start | bytes 208904 | tf_op jit(solution)/shard_map/ppermute | solution.py:287
  82.0 1.8 %collective-permute-start.27 = (f32[17,8,128]{2,1,0:T(8,128)S(1)}, f32[17,8,128]{2,1,0:T(8,128)S(1)}, u32[]{:S(2)}, u32[]{:S(2)}) collective-permute-start(f32[17,8,128]{2,1,0:T(8,128)S(1)} %get-tuple-element.56), channel_id=1, source_target_pairs={{0,2},{1,3},{2,4},{3,5},{4,6},{5,7},{6,0},{7,1},{8,10},{9,11},{10,... | collective-permute-start | bytes 208904 | tf_op jit(solution)/shard_map/ppermute | solution.py:287
  86.8 6.3 %collective-permute-done.26.refs_5_ = f32[17,8,128]{2,1,0:T(8,128)S(1)} collective-permute-done((f32[17,8,128]{2,1,0:T(8,128)S(1)}, f32[17,8,128]{2,1,0:T(8,128)S(1)}, u32[]{:S(2)}, u32[]{:S(2)}) %collective-permute-start.26) | collective-permute-done | bytes 69664 | tf_op jit(solution)/shard_map/ppermute | solution.py:287
  93.1 2.8 %collective-permute-done.28.refs_7_ = f32[17,8,128]{2,1,0:T(8,128)S(1)} collective-permute-done((f32[17,8,128]{2,1,0:T(8,128)S(1)}, f32[17,8,128]{2,1,0:T(8,128)S(1)}, u32[]{:S(2)}, u32[]{:S(2)}) %collective-permute-start.28) | collective-permute-done | bytes 69664 | tf_op jit(solution)/shard_map/ppermute | solution.py:287
  95.9 3.2 %shard_map.106 = (f32[1,16,128,128]{3,2,1,0:T(8,128)}, f32[1,768]{1,0:T(1,128)}) custom-call(s32[8]{0:T(128)S(1)} %stack.35.place_ref, s32[1]{0:T(128)} %bitcast.8.slab_ref, s32[1,768]{1,0:T(1,128)S(1)} %copy-done.3, bf16[128,128]{1,0:T(8,128)(2,1)S(1)} %dynamic-slice_bitcast_fusion.12.ty_ref, bf16[2,128,256]{2,1,0:T(8,128)(2,1)S(1)} %copy-done.1, ...), custom_call_target="tpu_custom_call" | custom-call | tf_op jit(solution)/shard_map/pallas_call | solution.py:314
  (66 shorter events, 19.9 us)
Async XLA Ops:
  7.0 6.8 %collective-permute-start.5 = (f32[2,2,128,128]{3,2,1,0:T(8,128)S(1)}, f32[2,2,128,128]{3,2,1,0:T(8,128)S(1)}, u32[]{:S(2)}, u32[]{:S(2)}) collective-permute-start(f32[2,2,128,128]{3,2,1,0:T(8,128)S(1)} %get-tuple-element.40), channel_id=1, source_target_pairs={{0,48},{8,200},{16,32},{24,216},{32,16},{40,232},{48,0},{56,248},{... | collective-permute-start | bytes 786440 | tf_op jit(solution)/shard_map/ppermute | solution.py:232
  12.6 6.8 %collective-permute-start.2 = (f32[2,2,128,128]{3,2,1,0:T(8,128)S(1)}, f32[2,2,128,128]{3,2,1,0:T(8,128)S(1)}, u32[]{:S(2)}, u32[]{:S(2)}) collective-permute-start(f32[2,2,128,128]{3,2,1,0:T(8,128)S(1)} %broadcast_select_fusion.8), channel_id=1, source_target_pairs={{0,48},{8,200},{16,32},{24,216},{32,16},{40,232},{48,0},{56,248},{... | collective-permute-start | bytes 786440 | tf_op jit(solution)/shard_map/ppermute | solution.py:232
  14.0 5.7 %collective-permute-start.6 = (f32[2,2,128,128]{3,2,1,0:T(8,128)S(1)}, f32[2,2,128,128]{3,2,1,0:T(8,128)S(1)}, u32[]{:S(2)}, u32[]{:S(2)}) collective-permute-start(f32[2,2,128,128]{3,2,1,0:T(8,128)S(1)} %broadcast_select_fusion.4), channel_id=1, source_target_pairs={{0,64},{8,24},{16,80},{24,8},{32,96},{40,56},{48,112},{56,40},{64,... | collective-permute-start | bytes 786440 | tf_op jit(solution)/shard_map/ppermute | solution.py:232
  19.8 6.8 %collective-permute-start.7 = (f32[2,2,128,128]{3,2,1,0:T(8,128)S(1)}, f32[2,2,128,128]{3,2,1,0:T(8,128)S(1)}, u32[]{:S(2)}, u32[]{:S(2)}) collective-permute-start(f32[2,2,128,128]{3,2,1,0:T(8,128)S(1)} %broadcast_select_fusion.5), channel_id=1, source_target_pairs={{0,192},{8,56},{16,208},{24,40},{32,224},{40,24},{48,240},{56,8},{... | collective-permute-start | bytes 786440 | tf_op jit(solution)/shard_map/ppermute | solution.py:232
  25.2 6.5 %collective-permute-start.4 = (f32[2,2,128,128]{3,2,1,0:T(8,128)S(1)}, f32[2,2,128,128]{3,2,1,0:T(8,128)S(1)}, u32[]{:S(2)}, u32[]{:S(2)}) collective-permute-start(f32[2,2,128,128]{3,2,1,0:T(8,128)S(1)} %broadcast_select_fusion.10), channel_id=1, source_target_pairs={{0,192},{8,56},{16,208},{24,40},{32,224},{40,24},{48,240},{56,8},{... | collective-permute-start | bytes 786440 | tf_op jit(solution)/shard_map/ppermute | solution.py:232
  31.9 7.2 %collective-permute-start.11 = (f32[2,2,128,128]{3,2,1,0:T(8,128)S(1)}, f32[2,2,128,128]{3,2,1,0:T(8,128)S(1)}, u32[]{:S(2)}, u32[]{:S(2)}) collective-permute-start(f32[2,2,128,128]{3,2,1,0:T(8,128)S(1)} %broadcast_select_fusion.11.refs_0_.refs_8_), channel_id=1, source_target_pairs={{0,16},{8,72},{16,0},{24,88},{32,48},{40,104},{48,32},{56,120},{64... | collective-permute-start | bytes 786440 | tf_op jit(solution)/shard_map/ppermute | solution.py:232
  32.1 10.3 %collective-permute-start.12 = (f32[2,2,128,128]{3,2,1,0:T(8,128)S(1)}, f32[2,2,128,128]{3,2,1,0:T(8,128)S(1)}, u32[]{:S(2)}, u32[]{:S(2)}) collective-permute-start(f32[2,2,128,128]{3,2,1,0:T(8,128)S(1)} %broadcast_select_fusion.7.refs_1_.refs_9_), channel_id=1, source_target_pairs={{0,48},{8,200},{16,32},{24,216},{32,16},{40,232},{48,0},{56,248},{... | collective-permute-start | bytes 786440 | tf_op jit(solution)/shard_map/ppermute | solution.py:232
  34.7 10.0 %collective-permute-start.9 = (f32[2,2,128,128]{3,2,1,0:T(8,128)S(1)}, f32[2,2,128,128]{3,2,1,0:T(8,128)S(1)}, u32[]{:S(2)}, u32[]{:S(2)}) collective-permute-start(f32[2,2,128,128]{3,2,1,0:T(8,128)S(1)} %broadcast_select_fusion.11.refs_0_.refs_8_), channel_id=1, source_target_pairs={{0,8},{8,0},{16,24},{24,16},{32,40},{40,32},{48,56},{56,48},{64,72... | collective-permute-start | bytes 786440 | tf_op jit(solution)/shard_map/ppermute | solution.py:232
  39.1 5.7 %collective-permute-start.10 = (f32[2,2,128,128]{3,2,1,0:T(8,128)S(1)}, f32[2,2,128,128]{3,2,1,0:T(8,128)S(1)}, u32[]{:S(2)}, u32[]{:S(2)}) collective-permute-start(f32[2,2,128,128]{3,2,1,0:T(8,128)S(1)} %broadcast_select_fusion.7.refs_1_.refs_9_), channel_id=1, source_target_pairs={{0,8},{8,0},{16,24},{24,16},{32,40},{40,32},{48,56},{56,48},{64,72... | collective-permute-start | bytes 786440 | tf_op jit(solution)/shard_map/ppermute | solution.py:232
  39.1 5.7 %collective-permute-start.13 = (f32[2,2,128,128]{3,2,1,0:T(8,128)S(1)}, f32[2,2,128,128]{3,2,1,0:T(8,128)S(1)}, u32[]{:S(2)}, u32[]{:S(2)}) collective-permute-start(f32[2,2,128,128]{3,2,1,0:T(8,128)S(1)} %collective-permute-done.11.refs_4_.refs_12_), channel_id=1, source_target_pairs={{0,8},{8,0},{16,24},{24,16},{32,40},{40,32},{48,56},{56,48},{64,72... | collective-permute-start | bytes 786440 | tf_op jit(solution)/shard_map/ppermute | solution.py:232
  47.6 11.7 %collective-permute-start.15 = (f32[16,8,128]{2,1,0:T(8,128)S(1)}, f32[16,8,128]{2,1,0:T(8,128)S(1)}, u32[]{:S(2)}, u32[]{:S(2)}) collective-permute-start(f32[16,8,128]{2,1,0:T(8,128)S(1)} %get-tuple-element.43), channel_id=1, source_target_pairs={{0,7},{1,0},{2,1},{3,2},{4,3},{5,4},{6,5},{7,6},{8,15},{9,8},{10,9... | collective-permute-start | bytes 196616 | tf_op jit(solution)/shard_map/ppermute | solution.py:287
  53.2 8.3 %collective-permute-start.16 = (f32[16,8,128]{2,1,0:T(8,128)S(1)}, f32[16,8,128]{2,1,0:T(8,128)S(1)}, u32[]{:S(2)}, u32[]{:S(2)}) collective-permute-start(f32[16,8,128]{2,1,0:T(8,128)S(1)} %get-tuple-element.44), channel_id=1, source_target_pairs={{0,6},{1,7},{2,0},{3,1},{4,2},{5,3},{6,4},{7,5},{8,14},{9,15},{10,... | collective-permute-start | bytes 196616 | tf_op jit(solution)/shard_map/ppermute | solution.py:287
  54.4 9.3 %collective-permute-start.17 = (f32[16,8,128]{2,1,0:T(8,128)S(1)}, f32[16,8,128]{2,1,0:T(8,128)S(1)}, u32[]{:S(2)}, u32[]{:S(2)}) collective-permute-start(f32[16,8,128]{2,1,0:T(8,128)S(1)} %get-tuple-element.45), channel_id=1, source_target_pairs={{0,5},{1,6},{2,7},{3,0},{4,1},{5,2},{6,3},{7,4},{8,13},{9,14},{10,... | collective-permute-start | bytes 196616 | tf_op jit(solution)/shard_map/ppermute | solution.py:287
  54.8 8.8 %collective-permute-start.18 = (f32[16,8,128]{2,1,0:T(8,128)S(1)}, f32[16,8,128]{2,1,0:T(8,128)S(1)}, u32[]{:S(2)}, u32[]{:S(2)}) collective-permute-start(f32[16,8,128]{2,1,0:T(8,128)S(1)} %get-tuple-element.46), channel_id=1, source_target_pairs={{0,4},{1,5},{2,6},{3,7},{4,0},{5,1},{6,2},{7,3},{8,12},{9,13},{10,... | collective-permute-start | bytes 196616 | tf_op jit(solution)/shard_map/ppermute | solution.py:287
  59.3 6.2 %collective-permute-start.19 = (f32[16,8,128]{2,1,0:T(8,128)S(1)}, f32[16,8,128]{2,1,0:T(8,128)S(1)}, u32[]{:S(2)}, u32[]{:S(2)}) collective-permute-start(f32[16,8,128]{2,1,0:T(8,128)S(1)} %get-tuple-element.47), channel_id=1, source_target_pairs={{0,3},{1,4},{2,5},{3,6},{4,7},{5,0},{6,1},{7,2},{8,11},{9,12},{10,... | collective-permute-start | bytes 196616 | tf_op jit(solution)/shard_map/ppermute | solution.py:287
  59.3 11.3 %collective-permute-start.20 = (f32[16,8,128]{2,1,0:T(8,128)S(1)}, f32[16,8,128]{2,1,0:T(8,128)S(1)}, u32[]{:S(2)}, u32[]{:S(2)}) collective-permute-start(f32[16,8,128]{2,1,0:T(8,128)S(1)} %get-tuple-element.48), channel_id=1, source_target_pairs={{0,2},{1,3},{2,4},{3,5},{4,6},{5,7},{6,0},{7,1},{8,10},{9,11},{10,... | collective-permute-start | bytes 196616 | tf_op jit(solution)/shard_map/ppermute | solution.py:287
  61.5 10.4 %collective-permute-start.21 = (f32[16,8,128]{2,1,0:T(8,128)S(1)}, f32[16,8,128]{2,1,0:T(8,128)S(1)}, u32[]{:S(2)}, u32[]{:S(2)}) collective-permute-start(f32[16,8,128]{2,1,0:T(8,128)S(1)} %get-tuple-element.49), channel_id=1, source_target_pairs={{0,1},{1,2},{2,3},{3,4},{4,5},{5,6},{6,7},{7,0},{8,9},{9,10},{10,1... | collective-permute-start | bytes 196616 | tf_op jit(solution)/shard_map/ppermute | solution.py:287
  73.1 8.9 %collective-permute-start.22 = (f32[17,8,128]{2,1,0:T(8,128)S(1)}, f32[17,8,128]{2,1,0:T(8,128)S(1)}, u32[]{:S(2)}, u32[]{:S(2)}) collective-permute-start(f32[17,8,128]{2,1,0:T(8,128)S(1)} %get-tuple-element.51), channel_id=1, source_target_pairs={{0,7},{1,0},{2,1},{3,2},{4,3},{5,4},{6,5},{7,6},{8,15},{9,8},{10,9... | collective-permute-start | bytes 208904 | tf_op jit(solution)/shard_map/ppermute | solution.py:287
  74.3 9.4 %collective-permute-start.23 = (f32[17,8,128]{2,1,0:T(8,128)S(1)}, f32[17,8,128]{2,1,0:T(8,128)S(1)}, u32[]{:S(2)}, u32[]{:S(2)}) collective-permute-start(f32[17,8,128]{2,1,0:T(8,128)S(1)} %get-tuple-element.52), channel_id=1, source_target_pairs={{0,6},{1,7},{2,0},{3,1},{4,2},{5,3},{6,4},{7,5},{8,14},{9,15},{10,... | collective-permute-start | bytes 208904 | tf_op jit(solution)/shard_map/ppermute | solution.py:287
  75.1 10.6 %collective-permute-start.24 = (f32[17,8,128]{2,1,0:T(8,128)S(1)}, f32[17,8,128]{2,1,0:T(8,128)S(1)}, u32[]{:S(2)}, u32[]{:S(2)}) collective-permute-start(f32[17,8,128]{2,1,0:T(8,128)S(1)} %get-tuple-element.53), channel_id=1, source_target_pairs={{0,5},{1,6},{2,7},{3,0},{4,1},{5,2},{6,3},{7,4},{8,13},{9,14},{10,... | collective-permute-start | bytes 208904 | tf_op jit(solution)/shard_map/ppermute | solution.py:287
  78.9 8.0 %collective-permute-start.25 = (f32[17,8,128]{2,1,0:T(8,128)S(1)}, f32[17,8,128]{2,1,0:T(8,128)S(1)}, u32[]{:S(2)}, u32[]{:S(2)}) collective-permute-start(f32[17,8,128]{2,1,0:T(8,128)S(1)} %get-tuple-element.54), channel_id=1, source_target_pairs={{0,4},{1,5},{2,6},{3,7},{4,0},{5,1},{6,2},{7,3},{8,12},{9,13},{10,... | collective-permute-start | bytes 208904 | tf_op jit(solution)/shard_map/ppermute | solution.py:287
  79.8 13.3 %collective-permute-start.26 = (f32[17,8,128]{2,1,0:T(8,128)S(1)}, f32[17,8,128]{2,1,0:T(8,128)S(1)}, u32[]{:S(2)}, u32[]{:S(2)}) collective-permute-start(f32[17,8,128]{2,1,0:T(8,128)S(1)} %get-tuple-element.55), channel_id=1, source_target_pairs={{0,3},{1,4},{2,5},{3,6},{4,7},{5,0},{6,1},{7,2},{8,11},{9,12},{10,... | collective-permute-start | bytes 208904 | tf_op jit(solution)/shard_map/ppermute | solution.py:287
  82.0 11.1 %collective-permute-start.27 = (f32[17,8,128]{2,1,0:T(8,128)S(1)}, f32[17,8,128]{2,1,0:T(8,128)S(1)}, u32[]{:S(2)}, u32[]{:S(2)}) collective-permute-start(f32[17,8,128]{2,1,0:T(8,128)S(1)} %get-tuple-element.56), channel_id=1, source_target_pairs={{0,2},{1,3},{2,4},{3,5},{4,6},{5,7},{6,0},{7,1},{8,10},{9,11},{10,... | collective-permute-start | bytes 208904 | tf_op jit(solution)/shard_map/ppermute | solution.py:287
  83.8 12.1 %collective-permute-start.28 = (f32[17,8,128]{2,1,0:T(8,128)S(1)}, f32[17,8,128]{2,1,0:T(8,128)S(1)}, u32[]{:S(2)}, u32[]{:S(2)}) collective-permute-start(f32[17,8,128]{2,1,0:T(8,128)S(1)} %get-tuple-element.57), channel_id=1, source_target_pairs={{0,1},{1,2},{2,3},{3,4},{4,5},{5,6},{6,7},{7,0},{8,9},{9,10},{10,1... | collective-permute-start | bytes 208904 | tf_op jit(solution)/shard_map/ppermute | solution.py:287
  (10 other events, 77.1 us)
where the time goes:
time: 99.4 us; the launch traced here: 99.1 us
  starting transfers between devices  49.5 us (50%)
  waiting for transfers between devices  36.5 us (37%)
  Pallas kernels  6.91 us (7%)
  local copies, waits for them, and re-layouts  4.32 us (4%)
    ppermute x14, starting transfers between devices, exchange_blocks(): came[SLABS - k] = lax.ppermute(blocks[k], 'slab', pairs)  27.1 us
    ppermute x14, starting transfers between devices, send(): lax.ppermute(value, 'band', CORE_PAIRS if name == 'swap' else cube_pairs(...  19.2 us
    ppermute x14, waiting for transfers between devices, exchange_blocks(): came[SLABS - k] = lax.ppermute(blocks[k], 'slab', pairs)  18.5 us
    ppermute x14, waiting for transfers between devices, send(): lax.ppermute(value, 'band', CORE_PAIRS if name == 'swap' else cube_pairs(...  17.2 us
    ppermute x1, starting transfers between devices, broadcast_sources(): lax.ppermute(lax.dynamic_index_in_dim(orbital, 1 - core, 0, keepdims=Fals...  3.29 us
    pallas_call x1, Pallas kernels, step(): call(inverse_kernel, [SMEM] * 2 + [VMEM] * (3 + SLABS + len(pieces)), (ja...  3.22 us
    pallas_call x1, Pallas kernels, step(): call(forward_kernel, [SMEM] + [VMEM] * (3 + len(pieces)), (block,) * SLABS)  2.49 us
    squeeze x3, local copies, waits for them, and re-layouts, turn(): return lax.dynamic_index_in_dim(tables, slab, 0, keepdims=False)  2.32 us
  transfers between devices with their start and end apart: 29, of which 14 were waited for; matrix products, arithmetic and copies ran while one was open for 3% of the time, Pallas kernels for 0%

commit v1 on v0

--- a/solution.py
+++ b/solution.py
@@ -135,7 +135,7 @@
             box = jnp.concatenate([ref[plane + q] for ref in back_refs], axis=0)
             rows.append(wide_product(ty_ref[...], box))
         high, low = bf16_parts(jnp.concatenate(rows, axis=0))
-        pots = dot(high, tz_ref[0]) + dot(low, tz_ref[0]) + dot(high, tz_ref[1])
+        pots = dot(jnp.concatenate([high, low], axis=1), tz_ref[: 2 * LANES]) + dot(high, tz_ref[2 * LANES :])
         value = piece_ref[0].reshape(2 * G, G) * pots[:, :G] + piece_ref[1].reshape(2 * G, G) * pots[:, G:]
         exchange_ref[0, pl.ds(plane, 2)] = value.reshape(2, G, G)
     power = jnp.concatenate([ref[PLANES] for ref in back_refs], axis=0)
@@ -201,11 +201,6 @@
     x = (me // 2) % 4
     y = me // 8
     code = gray(x) | (gray(y) << 2)
-    orbital = orbitals[0].reshape(2, 2, 2, 2, G, G)
-    mine = lax.dynamic_index_in_dim(orbital, core, 0, keepdims=False)
-    theirs = lax.ppermute(
-        lax.dynamic_index_in_dim(orbital, 1 - core, 0, keepdims=False), "band", CORE_PAIRS
-    )
     source_x = (source_ids // 2) % 4
     source_y = source_ids // 8
     relative = code ^ (gray(source_x) | (gray(source_y) << 2))
@@ -214,26 +209,33 @@
     def choose(slot, step):
         return jnp.where(flags[slot][step - 1], gots[slot], keeps[slot])
 
-    places, partner_places, sides = [], [], []
+    places, partner_places = [], []
     for slot in range(2):
         side = bit(code, (2 * core + slot) % 4)
-        sides.append(side)
         partner_side = bit(code, (2 * (1 - core) + slot) % 4)
         places.append((4 * core + 2 * slot + side, 4 * core + 2 * slot + 1 - side))
         base = 4 * (1 - core) + 2 * slot
         partner_places.append((base + partner_side, base + 1 - partner_side))
 
-    def half(slot, which):
-        own = lax.dynamic_index_in_dim(mine[slot], which, 0, keepdims=False)
-        other = lax.dynamic_index_in_dim(theirs[slot], which, 0, keepdims=False)
-        return jnp.where(is_mine, own[None], other[None])
+    def halves(orbitals, owner, away):
+        parts = []
+        for slot in range(2):
+            side = bit(code, (2 * owner + slot) % 4)
+            first = 8 * owner + 4 * slot + 2 * (1 - side if away else side)
+            parts.append(lax.dynamic_slice_in_dim(orbitals[0], first, 2, 0))
+        return parts
+
+    def begin(orbitals, away):
+        mine = halves(orbitals, core, away)
+        theirs = lax.ppermute(jnp.stack(halves(orbitals, 1 - core, away)), "band", CORE_PAIRS)
+        return [jnp.where(is_mine, mine[slot][None], theirs[slot][None]) for slot in range(2)]
 
     def send(slot, value, step, name):
         return lax.ppermute(value, "band", CORE_PAIRS if name == "swap" else cube_pairs(slot, step))
 
-    away = lax.optimization_barrier([half(slot, 1 - sides[slot]) for slot in range(2)])
+    away, later_orbitals = lax.optimization_barrier((begin(orbitals, True), orbitals))
     gots = [send(slot, away[slot], 0, "send") for slot in range(2)]
-    keeps = lax.optimization_barrier([half(slot, sides[slot]) for slot in range(2)])
+    keeps = list(lax.optimization_barrier(begin(later_orbitals, False)))
     flags = [
         [relative != 0] + [bit(relative, (2 * core + slot + step) % 4) == 1 for step in range(1, 4)]
         for slot in range(2)
@@ -295,7 +297,8 @@
     forward_x = turned(along_x, PLANES, 1, 0)
     inverse_x = turned(along_x.T, PLANES, 0, 1)
     inverse_y = turned(along_y.T, ROWS, 1, 1)
-    inverse_z = jnp.asarray(np.stack(split_table(along_z.T), axis=0))
+    high, low = split_table(along_z.T)
+    inverse_z = jnp.asarray(np.concatenate([high, high, low], axis=0))
 
     f32 = jnp.float32
     slab = lax.axis_index("slab").astype(jnp.int32)

time: 99.4 us -> 106 us (1.066)
  starting transfers between devices: 49.5 us -> 55.9 us
    ppermute x14, starting transfers between devices: 19.2 us -> 25 us  [send(): lax.ppermute(value, 'band', CORE_PAIRS if name == 'swap' else cube_pairs(...]
    squeeze x1 -> x0, local copies, waits for them, and re-layouts: 1.16 us -> none  [broadcast_sources(): lax.dynamic_index_in_dim(orbital, 1 - core, 0, keepdims=False)]
    broadcast_in_dim x2 -> x4, local copies, waits for them, and re-layouts: 0.08 us -> 1.22 us  [begin(): jnp.where(is_mine, mine[slot][None], theirs[slot][None])]
    ppermute x1 -> x2, starting transfers between devices: 3.29 us -> 3.75 us  [begin(): lax.ppermute(jnp.stack(halves(orbitals, 1 - core, away)), 'band', CORE_PA...]
  transfers between devices with their start and end apart: 29 -> 30, of which waited for: 14 -> 13; matrix products, arithmetic and copies ran while one was open for 3% -> 3% of each run, Pallas kernels for 0% -> 0%
where the time goes in v1:
time: 106 us; the launch traced here: 105 us
  starting transfers between devices  55.9 us (53%)
  waiting for transfers between devices  37.1 us (35%)
  Pallas kernels  6.71 us (6%)
  local copies, waits for them, and re-layouts  3.64 us (3%)
    ppermute x14, starting transfers between devices, exchange_blocks(): came[SLABS - k] = lax.ppermute(blocks[k], 'slab', pairs)  27.1 us
    ppermute x14, starting transfers between devices, send(): lax.ppermute(value, 'band', CORE_PAIRS if name == 'swap' else cube_pairs(...  25 us
    ppermute x14, waiting for transfers between devices, exchange_blocks(): came[SLABS - k] = lax.ppermute(blocks[k], 'slab', pairs)  18.5 us
    ppermute x14, waiting for transfers between devices, send(): lax.ppermute(value, 'band', CORE_PAIRS if name == 'swap' else cube_pairs(...  17.5 us
    ppermute x2, starting transfers between devices, begin(): lax.ppermute(jnp.stack(halves(orbitals, 1 - core, away)), 'band', CORE_PA...  3.75 us
    pallas_call x1, Pallas kernels, step(): call(inverse_kernel, [SMEM] * 2 + [VMEM] * (3 + SLABS + len(pieces)), (ja...  3.03 us
    pallas_call x1, Pallas kernels, step(): call(forward_kernel, [SMEM] + [VMEM] * (3 + len(pieces)), (block,) * SLABS)  2.49 us
    squeeze x3, local copies, waits for them, and re-layouts, turn(): return lax.dynamic_index_in_dim(tables, slab, 0, keepdims=False)  2.32 us
  transfers between devices with their start and end apart: 30, of which 13 were waited for; matrix products, arithmetic and copies ran while one was open for 3% of the time, Pallas kernels for 0%

profile of v1, /device:TPU:1, one launch (start us, length us, event | category | flops | bytes accessed | tf_op | source)
XLA Modules:
  0.0 105.3 jit_solution(14546951099284769786)
XLA Ops:
  2.0 3.3 %collective-permute-start = (f32[2,2,128,128]{3,2,1,0:T(8,128)S(1)}, f32[2,2,128,128]{3,2,1,0:T(8,128)S(1)}, u32[]{:S(2)}, u32[]{:S(2)}) collective-permute-start(f32[2,2,128,128]{3,2,1,0:T(8,128)S(1)} %pad_maximum_fusion), channel_id=1, source_target_pairs={{0,8},{8,0},{16,24},{24,16},{32,40},{40,32},{48,56},{56,48},{64,72... | collective-permute-start | bytes 786440 | tf_op jit(solution)/shard_map/ppermute | solution.py:230
  7.1 1.5 %collective-permute-start.6 = (f32[2,2,128,128]{3,2,1,0:T(8,128)S(1)}, f32[2,2,128,128]{3,2,1,0:T(8,128)S(1)}, u32[]{:S(2)}, u32[]{:S(2)}) collective-permute-start(f32[2,2,128,128]{3,2,1,0:T(8,128)S(1)} %get-tuple-element.42), channel_id=1, source_target_pairs={{0,48},{8,200},{16,32},{24,216},{32,16},{40,232},{48,0},{56,248},{... | collective-permute-start | bytes 786440 | tf_op jit(solution)/shard_map/ppermute | solution.py:234
  8.8 5.2 %collective-permute-done.6 = f32[2,2,128,128]{3,2,1,0:T(8,128)S(1)} collective-permute-done((f32[2,2,128,128]{3,2,1,0:T(8,128)S(1)}, f32[2,2,128,128]{3,2,1,0:T(8,128)S(1)}, u32[]{:S(2)}, u32[]{:S(2)}) %collective-permute-start.6) | collective-permute-done | bytes 262176 | tf_op jit(solution)/shard_map/ppermute | solution.py:234
  14.6 2.0 %collective-permute-start.3 = (f32[2,2,128,128]{3,2,1,0:T(8,128)S(1)}, f32[2,2,128,128]{3,2,1,0:T(8,128)S(1)}, u32[]{:S(2)}, u32[]{:S(2)}) collective-permute-start(f32[2,2,128,128]{3,2,1,0:T(8,128)S(1)} %broadcast_select_fusion.8), channel_id=1, source_target_pairs={{0,48},{8,200},{16,32},{24,216},{32,16},{40,232},{48,0},{56,248},{... | collective-permute-start | bytes 786440 | tf_op jit(solution)/shard_map/ppermute | solution.py:234
  16.6 3.0 %collective-permute-done.7 = f32[2,2,128,128]{3,2,1,0:T(8,128)S(1)} collective-permute-done((f32[2,2,128,128]{3,2,1,0:T(8,128)S(1)}, f32[2,2,128,128]{3,2,1,0:T(8,128)S(1)}, u32[]{:S(2)}, u32[]{:S(2)}) %collective-permute-start.7) | collective-permute-done | bytes 262176 | tf_op jit(solution)/shard_map/ppermute | solution.py:234
  19.7 2.1 %collective-permute-start.8 = (f32[2,2,128,128]{3,2,1,0:T(8,128)S(1)}, f32[2,2,128,128]{3,2,1,0:T(8,128)S(1)}, u32[]{:S(2)}, u32[]{:S(2)}) collective-permute-start(f32[2,2,128,128]{3,2,1,0:T(8,128)S(1)} %broadcast_select_fusion.5), channel_id=1, source_target_pairs={{0,192},{8,56},{16,208},{24,40},{32,224},{40,24},{48,240},{56,8},{... | collective-permute-start | bytes 786440 | tf_op jit(solution)/shard_map/ppermute | solution.py:234
  22.4 4.2 %collective-permute-done.8 = f32[2,2,128,128]{3,2,1,0:T(8,128)S(1)} collective-permute-done((f32[2,2,128,128]{3,2,1,0:T(8,128)S(1)}, f32[2,2,128,128]{3,2,1,0:T(8,128)S(1)}, u32[]{:S(2)}, u32[]{:S(2)}) %collective-permute-start.8) | collective-permute-done | bytes 262176 | tf_op jit(solution)/shard_map/ppermute | solution.py:234
  27.6 1.6 %collective-permute-start.5 = (f32[2,2,128,128]{3,2,1,0:T(8,128)S(1)}, f32[2,2,128,128]{3,2,1,0:T(8,128)S(1)}, u32[]{:S(2)}, u32[]{:S(2)}) collective-permute-start(f32[2,2,128,128]{3,2,1,0:T(8,128)S(1)} %broadcast_select_fusion.10), channel_id=1, source_target_pairs={{0,192},{8,56},{16,208},{24,40},{32,224},{40,24},{48,240},{56,8},{... | collective-permute-start | bytes 786440 | tf_op jit(solution)/shard_map/ppermute | solution.py:234
  29.2 4.2 %collective-permute-done.9 = f32[2,2,128,128]{3,2,1,0:T(8,128)S(1)} collective-permute-done((f32[2,2,128,128]{3,2,1,0:T(8,128)S(1)}, f32[2,2,128,128]{3,2,1,0:T(8,128)S(1)}, u32[]{:S(2)}, u32[]{:S(2)}) %collective-permute-start.9) | collective-permute-done | bytes 262176 | tf_op jit(solution)/shard_map/ppermute | solution.py:234
  33.5 3.0 %collective-permute-start.13 = (f32[2,2,128,128]{3,2,1,0:T(8,128)S(1)}, f32[2,2,128,128]{3,2,1,0:T(8,128)S(1)}, u32[]{:S(2)}, u32[]{:S(2)}) collective-permute-start(f32[2,2,128,128]{3,2,1,0:T(8,128)S(1)} %broadcast_select_fusion.7.refs_1_.refs_9_), channel_id=1, source_target_pairs={{0,48},{8,200},{16,32},{24,216},{32,16},{40,232},{48,0},{56,248},{... | collective-permute-start | bytes 786440 | tf_op jit(solution)/shard_map/ppermute | solution.py:234
  37.2 6.8 %collective-permute-start.11 = (f32[2,2,128,128]{3,2,1,0:T(8,128)S(1)}, f32[2,2,128,128]{3,2,1,0:T(8,128)S(1)}, u32[]{:S(2)}, u32[]{:S(2)}) collective-permute-start(f32[2,2,128,128]{3,2,1,0:T(8,128)S(1)} %broadcast_select_fusion.7.refs_1_.refs_9_), channel_id=1, source_target_pairs={{0,8},{8,0},{16,24},{24,16},{32,40},{40,32},{48,56},{56,48},{64,72... | collective-permute-start | bytes 786440 | tf_op jit(solution)/shard_map/ppermute | solution.py:234
  44.5 5.8 %collective-permute-start.14 = (f32[2,2,128,128]{3,2,1,0:T(8,128)S(1)}, f32[2,2,128,128]{3,2,1,0:T(8,128)S(1)}, u32[]{:S(2)}, u32[]{:S(2)}) collective-permute-start(f32[2,2,128,128]{3,2,1,0:T(8,128)S(1)} %collective-permute-done.12.refs_4_.refs_12_), channel_id=1, source_target_pairs={{0,8},{8,0},{16,24},{24,16},{32,40},{40,32},{48,56},{56,48},{64,72... | collective-permute-start | bytes 786440 | tf_op jit(solution)/shard_map/ppermute | solution.py:234
  51.4 2.5 %shard_map.104 = (f32[16,8,128]{2,1,0:T(8,128)S(1)}, f32[16,8,128]{2,1,0:T(8,128)S(1)}, f32[16,8,128]{2,1,0:T(8,128)S(1)}, f32[16,8,128]{2,1,0:T(8,128)S(1)}, f3...) custom-call(s32[8]{0:T(128)S(1)} %stack.45.place_ref, ...), custom_call_target="tpu_custom_call" | custom-call | tf_op jit(solution)/shard_map/pallas_call | solution.py:308
  53.9 5.7 %collective-permute-start.16 = (f32[16,8,128]{2,1,0:T(8,128)S(1)}, f32[16,8,128]{2,1,0:T(8,128)S(1)}, u32[]{:S(2)}, u32[]{:S(2)}) collective-permute-start(f32[16,8,128]{2,1,0:T(8,128)S(1)} %get-tuple-element.45), channel_id=1, source_target_pairs={{0,7},{1,0},{2,1},{3,2},{4,3},{5,4},{6,5},{7,6},{8,15},{9,8},{10,9... | collective-permute-start | bytes 196616 | tf_op jit(solution)/shard_map/ppermute | solution.py:289
  61.3 4.5 %collective-permute-start.19 = (f32[16,8,128]{2,1,0:T(8,128)S(1)}, f32[16,8,128]{2,1,0:T(8,128)S(1)}, u32[]{:S(2)}, u32[]{:S(2)}) collective-permute-start(f32[16,8,128]{2,1,0:T(8,128)S(1)} %get-tuple-element.48), channel_id=1, source_target_pairs={{0,4},{1,5},{2,6},{3,7},{4,0},{5,1},{6,2},{7,3},{8,12},{9,13},{10,... | collective-permute-start | bytes 196616 | tf_op jit(solution)/shard_map/ppermute | solution.py:289
  65.8 2.3 %collective-permute-start.21 = (f32[16,8,128]{2,1,0:T(8,128)S(1)}, f32[16,8,128]{2,1,0:T(8,128)S(1)}, u32[]{:S(2)}, u32[]{:S(2)}) collective-permute-start(f32[16,8,128]{2,1,0:T(8,128)S(1)} %get-tuple-element.50), channel_id=1, source_target_pairs={{0,2},{1,3},{2,4},{3,5},{4,6},{5,7},{6,0},{7,1},{8,10},{9,11},{10,... | collective-permute-start | bytes 196616 | tf_op jit(solution)/shard_map/ppermute | solution.py:289
  70.1 1.8 %collective-permute-done.20.refs_5_ = f32[16,8,128]{2,1,0:T(8,128)S(1)} collective-permute-done((f32[16,8,128]{2,1,0:T(8,128)S(1)}, f32[16,8,128]{2,1,0:T(8,128)S(1)}, u32[]{:S(2)}, u32[]{:S(2)}) %collective-permute-start.20) | collective-permute-done | bytes 65568 | tf_op jit(solution)/shard_map/ppermute | solution.py:289
  71.9 5.1 %collective-permute-done.21.refs_6_ = f32[16,8,128]{2,1,0:T(8,128)S(1)} collective-permute-done((f32[16,8,128]{2,1,0:T(8,128)S(1)}, f32[16,8,128]{2,1,0:T(8,128)S(1)}, u32[]{:S(2)}, u32[]{:S(2)}) %collective-permute-start.21) | collective-permute-done | bytes 65568 | tf_op jit(solution)/shard_map/ppermute | solution.py:289
  81.5 3.8 %collective-permute-start.25 = (f32[17,8,128]{2,1,0:T(8,128)S(1)}, f32[17,8,128]{2,1,0:T(8,128)S(1)}, u32[]{:S(2)}, u32[]{:S(2)}) collective-permute-start(f32[17,8,128]{2,1,0:T(8,128)S(1)} %get-tuple-element.55), channel_id=1, source_target_pairs={{0,5},{1,6},{2,7},{3,0},{4,1},{5,2},{6,3},{7,4},{8,13},{9,14},{10,... | collective-permute-start | bytes 208904 | tf_op jit(solution)/shard_map/ppermute | solution.py:289
  86.3 2.2 %collective-permute-start.27 = (f32[17,8,128]{2,1,0:T(8,128)S(1)}, f32[17,8,128]{2,1,0:T(8,128)S(1)}, u32[]{:S(2)}, u32[]{:S(2)}) collective-permute-start(f32[17,8,128]{2,1,0:T(8,128)S(1)} %get-tuple-element.57), channel_id=1, source_target_pairs={{0,3},{1,4},{2,5},{3,6},{4,7},{5,0},{6,1},{7,2},{8,11},{9,12},{10,... | collective-permute-start | bytes 208904 | tf_op jit(solution)/shard_map/ppermute | solution.py:289
  88.4 1.8 %collective-permute-start.28 = (f32[17,8,128]{2,1,0:T(8,128)S(1)}, f32[17,8,128]{2,1,0:T(8,128)S(1)}, u32[]{:S(2)}, u32[]{:S(2)}) collective-permute-start(f32[17,8,128]{2,1,0:T(8,128)S(1)} %get-tuple-element.58), channel_id=1, source_target_pairs={{0,2},{1,3},{2,4},{3,5},{4,6},{5,7},{6,0},{7,1},{8,10},{9,11},{10,... | collective-permute-start | bytes 208904 | tf_op jit(solution)/shard_map/ppermute | solution.py:289
  93.3 6.3 %collective-permute-done.27.refs_5_ = f32[17,8,128]{2,1,0:T(8,128)S(1)} collective-permute-done((f32[17,8,128]{2,1,0:T(8,128)S(1)}, f32[17,8,128]{2,1,0:T(8,128)S(1)}, u32[]{:S(2)}, u32[]{:S(2)}) %collective-permute-start.27) | collective-permute-done | bytes 69664 | tf_op jit(solution)/shard_map/ppermute | solution.py:289
  99.6 2.7 %collective-permute-done.29.refs_7_ = f32[17,8,128]{2,1,0:T(8,128)S(1)} collective-permute-done((f32[17,8,128]{2,1,0:T(8,128)S(1)}, f32[17,8,128]{2,1,0:T(8,128)S(1)}, u32[]{:S(2)}, u32[]{:S(2)}) %collective-permute-start.29) | collective-permute-done | bytes 69664 | tf_op jit(solution)/shard_map/ppermute | solution.py:289
  102.3 3.0 %shard_map.106 = (f32[1,16,128,128]{3,2,1,0:T(8,128)}, f32[1,768]{1,0:T(1,128)}) custom-call(s32[8]{0:T(128)S(1)} %stack.45.place_ref, s32[1]{0:T(128)} %bitcast.8.slab_ref, s32[1,768]{1,0:T(1,128)S(1)} %copy-done.3, bf16[128,128]{1,0:T(8,128)(2,1)S(1)} %dynamic-slice_bitcast_fusion.7.ty_ref, bf16[384,256]{1,0:T(8,128)(2,1)S(1)} %copy-done.1, ...), custom_call_target="tpu_custom_call" | custom-call | tf_op jit(solution)/shard_map/pallas_call | solution.py:317
  (71 shorter events, 20.1 us)
Async XLA Ops:
  7.1 7.4 %collective-permute-start.1 = (f32[2,2,128,128]{3,2,1,0:T(8,128)S(1)}, f32[2,2,128,128]{3,2,1,0:T(8,128)S(1)}, u32[]{:S(2)}, u32[]{:S(2)}) collective-permute-start(f32[2,2,128,128]{3,2,1,0:T(8,128)S(1)} %get-tuple-element.35), channel_id=1, source_target_pairs={{0,16},{8,72},{16,0},{24,88},{32,48},{40,104},{48,32},{56,120},{64... | collective-permute-start | bytes 786440 | tf_op jit(solution)/shard_map/ppermute | solution.py:234
  7.1 6.8 %collective-permute-start.6 = (f32[2,2,128,128]{3,2,1,0:T(8,128)S(1)}, f32[2,2,128,128]{3,2,1,0:T(8,128)S(1)}, u32[]{:S(2)}, u32[]{:S(2)}) collective-permute-start(f32[2,2,128,128]{3,2,1,0:T(8,128)S(1)} %get-tuple-element.42), channel_id=1, source_target_pairs={{0,48},{8,200},{16,32},{24,216},{32,16},{40,232},{48,0},{56,248},{... | collective-permute-start | bytes 786440 | tf_op jit(solution)/shard_map/ppermute | solution.py:234
  14.6 7.2 %collective-permute-start.3 = (f32[2,2,128,128]{3,2,1,0:T(8,128)S(1)}, f32[2,2,128,128]{3,2,1,0:T(8,128)S(1)}, u32[]{:S(2)}, u32[]{:S(2)}) collective-permute-start(f32[2,2,128,128]{3,2,1,0:T(8,128)S(1)} %broadcast_select_fusion.8), channel_id=1, source_target_pairs={{0,48},{8,200},{16,32},{24,216},{32,16},{40,232},{48,0},{56,248},{... | collective-permute-start | bytes 786440 | tf_op jit(solution)/shard_map/ppermute | solution.py:234
  19.7 6.9 %collective-permute-start.8 = (f32[2,2,128,128]{3,2,1,0:T(8,128)S(1)}, f32[2,2,128,128]{3,2,1,0:T(8,128)S(1)}, u32[]{:S(2)}, u32[]{:S(2)}) collective-permute-start(f32[2,2,128,128]{3,2,1,0:T(8,128)S(1)} %broadcast_select_fusion.5), channel_id=1, source_target_pairs={{0,192},{8,56},{16,208},{24,40},{32,224},{40,24},{48,240},{56,8},{... | collective-permute-start | bytes 786440 | tf_op jit(solution)/shard_map/ppermute | solution.py:234
  27.6 8.9 %collective-permute-start.5 = (f32[2,2,128,128]{3,2,1,0:T(8,128)S(1)}, f32[2,2,128,128]{3,2,1,0:T(8,128)S(1)}, u32[]{:S(2)}, u32[]{:S(2)}) collective-permute-start(f32[2,2,128,128]{3,2,1,0:T(8,128)S(1)} %broadcast_select_fusion.10), channel_id=1, source_target_pairs={{0,192},{8,56},{16,208},{24,40},{32,224},{40,24},{48,240},{56,8},{... | collective-permute-start | bytes 786440 | tf_op jit(solution)/shard_map/ppermute | solution.py:234
  33.5 10.6 %collective-permute-start.13 = (f32[2,2,128,128]{3,2,1,0:T(8,128)S(1)}, f32[2,2,128,128]{3,2,1,0:T(8,128)S(1)}, u32[]{:S(2)}, u32[]{:S(2)}) collective-permute-start(f32[2,2,128,128]{3,2,1,0:T(8,128)S(1)} %broadcast_select_fusion.7.refs_1_.refs_9_), channel_id=1, source_target_pairs={{0,48},{8,200},{16,32},{24,216},{32,16},{40,232},{48,0},{56,248},{... | collective-permute-start | bytes 786440 | tf_op jit(solution)/shard_map/ppermute | solution.py:234
  36.6 8.0 %collective-permute-start.12 = (f32[2,2,128,128]{3,2,1,0:T(8,128)S(1)}, f32[2,2,128,128]{3,2,1,0:T(8,128)S(1)}, u32[]{:S(2)}, u32[]{:S(2)}) collective-permute-start(f32[2,2,128,128]{3,2,1,0:T(8,128)S(1)} %broadcast_select_fusion.11.refs_0_.refs_8_), channel_id=1, source_target_pairs={{0,16},{8,72},{16,0},{24,88},{32,48},{40,104},{48,32},{56,120},{64... | collective-permute-start | bytes 786440 | tf_op jit(solution)/shard_map/ppermute | solution.py:234
  37.2 13.9 %collective-permute-start.11 = (f32[2,2,128,128]{3,2,1,0:T(8,128)S(1)}, f32[2,2,128,128]{3,2,1,0:T(8,128)S(1)}, u32[]{:S(2)}, u32[]{:S(2)}) collective-permute-start(f32[2,2,128,128]{3,2,1,0:T(8,128)S(1)} %broadcast_select_fusion.7.refs_1_.refs_9_), channel_id=1, source_target_pairs={{0,8},{8,0},{16,24},{24,16},{32,40},{40,32},{48,56},{56,48},{64,72... | collective-permute-start | bytes 786440 | tf_op jit(solution)/shard_map/ppermute | solution.py:234
  44.0 7.1 %collective-permute-start.10 = (f32[2,2,128,128]{3,2,1,0:T(8,128)S(1)}, f32[2,2,128,128]{3,2,1,0:T(8,128)S(1)}, u32[]{:S(2)}, u32[]{:S(2)}) collective-permute-start(f32[2,2,128,128]{3,2,1,0:T(8,128)S(1)} %broadcast_select_fusion.11.refs_0_.refs_8_), channel_id=1, source_target_pairs={{0,8},{8,0},{16,24},{24,16},{32,40},{40,32},{48,56},{56,48},{64,72... | collective-permute-start | bytes 786440 | tf_op jit(solution)/shard_map/ppermute | solution.py:234
  44.1 7.0 %collective-permute-start.15 = (f32[2,2,128,128]{3,2,1,0:T(8,128)S(1)}, f32[2,2,128,128]{3,2,1,0:T(8,128)S(1)}, u32[]{:S(2)}, u32[]{:S(2)}) collective-permute-start(f32[2,2,128,128]{3,2,1,0:T(8,128)S(1)} %collective-permute-done.13.refs_5_.refs_13_), channel_id=1, source_target_pairs={{0,8},{8,0},{16,24},{24,16},{32,40},{40,32},{48,56},{56,48},{64,72... | collective-permute-start | bytes 786440 | tf_op jit(solution)/shard_map/ppermute | solution.py:234
  44.5 6.9 %collective-permute-start.14 = (f32[2,2,128,128]{3,2,1,0:T(8,128)S(1)}, f32[2,2,128,128]{3,2,1,0:T(8,128)S(1)}, u32[]{:S(2)}, u32[]{:S(2)}) collective-permute-start(f32[2,2,128,128]{3,2,1,0:T(8,128)S(1)} %collective-permute-done.12.refs_4_.refs_12_), channel_id=1, source_target_pairs={{0,8},{8,0},{16,24},{24,16},{32,40},{40,32},{48,56},{56,48},{64,72... | collective-permute-start | bytes 786440 | tf_op jit(solution)/shard_map/ppermute | solution.py:234
  53.9 11.8 %collective-permute-start.16 = (f32[16,8,128]{2,1,0:T(8,128)S(1)}, f32[16,8,128]{2,1,0:T(8,128)S(1)}, u32[]{:S(2)}, u32[]{:S(2)}) collective-permute-start(f32[16,8,128]{2,1,0:T(8,128)S(1)} %get-tuple-element.45), channel_id=1, source_target_pairs={{0,7},{1,0},{2,1},{3,2},{4,3},{5,4},{6,5},{7,6},{8,15},{9,8},{10,9... | collective-permute-start | bytes 196616 | tf_op jit(solution)/shard_map/ppermute | solution.py:289
  59.7 8.5 %collective-permute-start.17 = (f32[16,8,128]{2,1,0:T(8,128)S(1)}, f32[16,8,128]{2,1,0:T(8,128)S(1)}, u32[]{:S(2)}, u32[]{:S(2)}) collective-permute-start(f32[16,8,128]{2,1,0:T(8,128)S(1)} %get-tuple-element.46), channel_id=1, source_target_pairs={{0,6},{1,7},{2,0},{3,1},{4,2},{5,3},{6,4},{7,5},{8,14},{9,15},{10,... | collective-permute-start | bytes 196616 | tf_op jit(solution)/shard_map/ppermute | solution.py:289
  60.8 9.3 %collective-permute-start.18 = (f32[16,8,128]{2,1,0:T(8,128)S(1)}, f32[16,8,128]{2,1,0:T(8,128)S(1)}, u32[]{:S(2)}, u32[]{:S(2)}) collective-permute-start(f32[16,8,128]{2,1,0:T(8,128)S(1)} %get-tuple-element.47), channel_id=1, source_target_pairs={{0,5},{1,6},{2,7},{3,0},{4,1},{5,2},{6,3},{7,4},{8,13},{9,14},{10,... | collective-permute-start | bytes 196616 | tf_op jit(solution)/shard_map/ppermute | solution.py:289
  61.3 8.8 %collective-permute-start.19 = (f32[16,8,128]{2,1,0:T(8,128)S(1)}, f32[16,8,128]{2,1,0:T(8,128)S(1)}, u32[]{:S(2)}, u32[]{:S(2)}) collective-permute-start(f32[16,8,128]{2,1,0:T(8,128)S(1)} %get-tuple-element.48), channel_id=1, source_target_pairs={{0,4},{1,5},{2,6},{3,7},{4,0},{5,1},{6,2},{7,3},{8,12},{9,13},{10,... | collective-permute-start | bytes 196616 | tf_op jit(solution)/shard_map/ppermute | solution.py:289
  65.8 11.3 %collective-permute-start.21 = (f32[16,8,128]{2,1,0:T(8,128)S(1)}, f32[16,8,128]{2,1,0:T(8,128)S(1)}, u32[]{:S(2)}, u32[]{:S(2)}) collective-permute-start(f32[16,8,128]{2,1,0:T(8,128)S(1)} %get-tuple-element.50), channel_id=1, source_target_pairs={{0,2},{1,3},{2,4},{3,5},{4,6},{5,7},{6,0},{7,1},{8,10},{9,11},{10,... | collective-permute-start | bytes 196616 | tf_op jit(solution)/shard_map/ppermute | solution.py:289
  68.1 10.3 %collective-permute-start.22 = (f32[16,8,128]{2,1,0:T(8,128)S(1)}, f32[16,8,128]{2,1,0:T(8,128)S(1)}, u32[]{:S(2)}, u32[]{:S(2)}) collective-permute-start(f32[16,8,128]{2,1,0:T(8,128)S(1)} %get-tuple-element.51), channel_id=1, source_target_pairs={{0,1},{1,2},{2,3},{3,4},{4,5},{5,6},{6,7},{7,0},{8,9},{9,10},{10,1... | collective-permute-start | bytes 196616 | tf_op jit(solution)/shard_map/ppermute | solution.py:289
  79.6 8.9 %collective-permute-start.23 = (f32[17,8,128]{2,1,0:T(8,128)S(1)}, f32[17,8,128]{2,1,0:T(8,128)S(1)}, u32[]{:S(2)}, u32[]{:S(2)}) collective-permute-start(f32[17,8,128]{2,1,0:T(8,128)S(1)} %get-tuple-element.53), channel_id=1, source_target_pairs={{0,7},{1,0},{2,1},{3,2},{4,3},{5,4},{6,5},{7,6},{8,15},{9,8},{10,9... | collective-permute-start | bytes 208904 | tf_op jit(solution)/shard_map/ppermute | solution.py:289
  80.8 9.4 %collective-permute-start.24 = (f32[17,8,128]{2,1,0:T(8,128)S(1)}, f32[17,8,128]{2,1,0:T(8,128)S(1)}, u32[]{:S(2)}, u32[]{:S(2)}) collective-permute-start(f32[17,8,128]{2,1,0:T(8,128)S(1)} %get-tuple-element.54), channel_id=1, source_target_pairs={{0,6},{1,7},{2,0},{3,1},{4,2},{5,3},{6,4},{7,5},{8,14},{9,15},{10,... | collective-permute-start | bytes 208904 | tf_op jit(solution)/shard_map/ppermute | solution.py:289
  81.5 10.6 %collective-permute-start.25 = (f32[17,8,128]{2,1,0:T(8,128)S(1)}, f32[17,8,128]{2,1,0:T(8,128)S(1)}, u32[]{:S(2)}, u32[]{:S(2)}) collective-permute-start(f32[17,8,128]{2,1,0:T(8,128)S(1)} %get-tuple-element.55), channel_id=1, source_target_pairs={{0,5},{1,6},{2,7},{3,0},{4,1},{5,2},{6,3},{7,4},{8,13},{9,14},{10,... | collective-permute-start | bytes 208904 | tf_op jit(solution)/shard_map/ppermute | solution.py:289
  85.4 8.0 %collective-permute-start.26 = (f32[17,8,128]{2,1,0:T(8,128)S(1)}, f32[17,8,128]{2,1,0:T(8,128)S(1)}, u32[]{:S(2)}, u32[]{:S(2)}) collective-permute-start(f32[17,8,128]{2,1,0:T(8,128)S(1)} %get-tuple-element.56), channel_id=1, source_target_pairs={{0,4},{1,5},{2,6},{3,7},{4,0},{5,1},{6,2},{7,3},{8,12},{9,13},{10,... | collective-permute-start | bytes 208904 | tf_op jit(solution)/shard_map/ppermute | solution.py:289
  86.3 13.3 %collective-permute-start.27 = (f32[17,8,128]{2,1,0:T(8,128)S(1)}, f32[17,8,128]{2,1,0:T(8,128)S(1)}, u32[]{:S(2)}, u32[]{:S(2)}) collective-permute-start(f32[17,8,128]{2,1,0:T(8,128)S(1)} %get-tuple-element.57), channel_id=1, source_target_pairs={{0,3},{1,4},{2,5},{3,6},{4,7},{5,0},{6,1},{7,2},{8,11},{9,12},{10,... | collective-permute-start | bytes 208904 | tf_op jit(solution)/shard_map/ppermute | solution.py:289
  88.4 11.2 %collective-permute-start.28 = (f32[17,8,128]{2,1,0:T(8,128)S(1)}, f32[17,8,128]{2,1,0:T(8,128)S(1)}, u32[]{:S(2)}, u32[]{:S(2)}) collective-permute-start(f32[17,8,128]{2,1,0:T(8,128)S(1)} %get-tuple-element.58), channel_id=1, source_target_pairs={{0,2},{1,3},{2,4},{3,5},{4,6},{5,7},{6,0},{7,1},{8,10},{9,11},{10,... | collective-permute-start | bytes 208904 | tf_op jit(solution)/shard_map/ppermute | solution.py:289
  90.2 12.1 %collective-permute-start.29 = (f32[17,8,128]{2,1,0:T(8,128)S(1)}, f32[17,8,128]{2,1,0:T(8,128)S(1)}, u32[]{:S(2)}, u32[]{:S(2)}) collective-permute-start(f32[17,8,128]{2,1,0:T(8,128)S(1)} %get-tuple-element.59), channel_id=1, source_target_pairs={{0,1},{1,2},{2,3},{3,4},{4,5},{5,6},{6,7},{7,0},{8,9},{9,10},{10,1... | collective-permute-start | bytes 208904 | tf_op jit(solution)/shard_map/ppermute | solution.py:289
  (11 other events, 89.5 us)

commit v2 on v1

--- a/solution.py
+++ b/solution.py
@@ -15,6 +15,7 @@
 SLOTS = 768
 ROWS = 8
 LANES = 128
+SENT = 7
 
 
 def split_table(table):
@@ -66,8 +67,25 @@
     return dot(table, jnp.concatenate([high, high, low], axis=0))
 
 
-def forward_kernel(place_ref, orbital_ref, ty_ref, tz_ref, *refs):
-    piece_refs, out_refs = refs[:-SLABS], refs[-SLABS:]
+def sent_blocks(refs):
+    home, pair, two, three, five, six, seven = refs
+    return [home, pair.at[0], two, three, pair.at[1], five, six, seven]
+
+
+def came_blocks(refs):
+    home, one, two, three, far, six, near = refs
+    return [home, one, two, three, far.at[1], far.at[0], six, near.at[0]]
+
+
+def by_slab(steps, up):
+    return [
+        steps[k] if k % 4 == 0 else jnp.where(up, steps[k], steps[SLABS - k]) for k in range(SLABS)
+    ]
+
+
+def forward_kernel(place_ref, core_ref, orbital_ref, ty_ref, tz_ref, *refs):
+    piece_refs, out_refs = refs[:-SENT], sent_blocks(refs[-SENT:])
+    up = core_ref[0] == 1
     for p, piece_ref in enumerate(piece_refs):
         plane = place_ref[p] * 2
         orbital = orbital_ref[0, pl.ds(plane, 2)]
@@ -78,15 +96,17 @@
         along_z = first[:, :LANES] + first[:, LANES:] + dot(low, tz_ref[:, :LANES])
         for q in range(2):
             box = left_product(ty_ref[...], along_z[q * G : (q + 1) * G])
+            blocks = by_slab([box[k * ROWS : (k + 1) * ROWS] for k in range(SLABS)], up)
             for k in range(SLABS):
-                out_refs[k][plane + q] = box[k * ROWS : (k + 1) * ROWS]
-
-
-def filter_kernel(slab_ref, tx_ref, txt_ref, *refs):
-    cols_refs, out_refs = refs[:SLABS], refs[SLABS:]
+                out_refs[k][plane + q] = blocks[k]
+
+
+def filter_kernel(slab_ref, core_ref, tx_ref, txt_ref, *refs):
+    cols_refs, out_refs = came_blocks(refs[:SENT]), sent_blocks(refs[SENT:])
+    up = core_ref[0] == 1
 
     def columns(j):
-        return jnp.concatenate([ref[:, j, :] for ref in cols_refs], axis=0)
+        return jnp.concatenate(by_slab([ref[:, j, :] for ref in cols_refs], up), axis=0)
 
     lane = lax.broadcasted_iota(jnp.int32, (2 * KCUT, LANES), 1)
     row = lax.broadcasted_iota(jnp.int32, (2 * KCUT, LANES), 0)
@@ -119,26 +139,29 @@
         power_rows.append(jnp.where(first, same, pltpu.roll(other, 32, 1)) * (1.0 / 64.0))
         for k, value in ((j, cos_y), (j + 4, sin_y)):
             back = wide_product(txt_ref[...], spread * value)
+            blocks = by_slab([back[d * PLANES : (d + 1) * PLANES] for d in range(SLABS)], up)
             for d in range(SLABS):
-                out_refs[d][0:PLANES, k, :] = back[d * PLANES : (d + 1) * PLANES]
+                out_refs[d][0:PLANES, k, :] = blocks[d]
     power = jnp.concatenate(power_rows + power_rows, axis=0)
     for d in range(SLABS):
         out_refs[d][PLANES] = power
 
 
-def inverse_kernel(place_ref, slab_ref, ids_ref, ty_ref, tz_ref, *refs):
-    back_refs, piece_refs, exchange_ref, energy_ref = refs[:SLABS], refs[SLABS:-2], refs[-2], refs[-1]
+def inverse_kernel(place_ref, slab_ref, core_ref, ids_ref, ty_ref, tz_ref, *refs):
+    back_refs, piece_refs, exchange_ref, energy_ref = refs[:SENT], refs[SENT:-2], refs[-2], refs[-1]
+    back_refs = came_blocks(back_refs)
+    up = core_ref[0] == 1
     for p, piece_ref in enumerate(piece_refs):
         plane = place_ref[p] * 2
         rows = []
         for q in range(2):
-            box = jnp.concatenate([ref[plane + q] for ref in back_refs], axis=0)
+            box = jnp.concatenate(by_slab([ref[plane + q] for ref in back_refs], up), axis=0)
             rows.append(wide_product(ty_ref[...], box))
         high, low = bf16_parts(jnp.concatenate(rows, axis=0))
         pots = dot(jnp.concatenate([high, low], axis=1), tz_ref[: 2 * LANES]) + dot(high, tz_ref[2 * LANES :])
         value = piece_ref[0].reshape(2 * G, G) * pots[:, :G] + piece_ref[1].reshape(2 * G, G) * pots[:, G:]
         exchange_ref[0, pl.ds(plane, 2)] = value.reshape(2, G, G)
-    power = jnp.concatenate([ref[PLANES] for ref in back_refs], axis=0)
+    power = jnp.concatenate(by_slab([ref[PLANES] for ref in back_refs], up), axis=0)
     ids = ids_ref[...]
     wave_y = ids // 64 - KCUT
     wave_z = ids % 64 - KCUT
@@ -279,15 +302,29 @@
     return lax.dynamic_index_in_dim(tables, slab, 0, keepdims=False)
 
 
-FAR_ORDER = (4, 3, 5, 2, 6, 1, 7)
-
-
 def exchange_blocks(blocks):
-    came = [blocks[0]] + [None] * (SLABS - 1)
-    for k in FAR_ORDER:
-        pairs = [(z, (z + k) % SLABS) for z in range(SLABS)]
-        came[SLABS - k] = lax.ppermute(blocks[k], "slab", pairs)
-    return came
+    home, pair, two, three, five, six, seven = blocks
+
+    def send(value, steps):
+        pairs = []
+        for band in range(32):
+            ahead = steps if band % 2 else -steps
+            for z in range(SLABS):
+                pairs.append((band * SLABS + z, band * SLABS + (z + ahead) % SLABS))
+        return lax.ppermute(value, ("band", "slab"), pairs)
+
+    near = send(pair, 1)
+    three_back = send(five, -3)
+    far = send(jnp.stack([three, near[1]]), 3)
+    six_here = send(two, 2)
+    two_here = send(six, -2)
+    one_here = send(seven, -1)
+    return [home, one_here, two_here, three_back, far, six_here, near]
+
+
+def sent_shapes(block):
+    pair = jax.ShapeDtypeStruct((2,) + block.shape, block.dtype)
+    return (block, pair) + (block,) * 5
 
 
 def step(orbitals, column_ids, source_ids):
@@ -305,23 +342,24 @@
     slab_ref = slab.reshape(1)
     pieces, places = broadcast_sources(orbitals, source_ids)
     block = jax.ShapeDtypeStruct((PLANES, ROWS, LANES), f32)
+    core = (lax.axis_index("band") % 2).astype(jnp.int32).reshape(1)
     columns = call(
-        forward_kernel, [SMEM] + [VMEM] * (3 + len(pieces)), (block,) * SLABS
-    )(places, orbitals, turn(forward_y, slab), forward_z, *pieces)
+        forward_kernel, [SMEM] * 2 + [VMEM] * (3 + len(pieces)), sent_shapes(block)
+    )(places, core, orbitals, turn(forward_y, slab), forward_z, *pieces)
     columns = exchange_blocks(columns)
     block = jax.ShapeDtypeStruct((PLANES + 1, ROWS, LANES), f32)
     back = call(
-        filter_kernel, [SMEM] + [VMEM] * (2 + SLABS), (block,) * SLABS
-    )(slab_ref, turn(forward_x, slab), turn(inverse_x, slab), *columns)
+        filter_kernel, [SMEM] * 2 + [VMEM] * (2 + SENT), sent_shapes(block)
+    )(slab_ref, core, turn(forward_x, slab), turn(inverse_x, slab), *columns)
     back = exchange_blocks(back)
     exchange, energy = call(
         inverse_kernel,
-        [SMEM] * 2 + [VMEM] * (3 + SLABS + len(pieces)),
+        [SMEM] * 3 + [VMEM] * (3 + SENT + len(pieces)),
         (
             jax.ShapeDtypeStruct((1, PLANES, G, G), f32),
             jax.ShapeDtypeStruct((1, SLOTS), f32),
         ),
-    )(places, slab_ref, column_ids, turn(inverse_y, slab), inverse_z, *back, *pieces)
+    )(places, slab_ref, core, column_ids, turn(inverse_y, slab), inverse_z, *back, *pieces)
     return exchange, energy
 
 

time: 106 us -> 102 us (0.962)
  the two profiles are of different devices: /device:TPU:1 before, /device:TPU:64 now
where the time goes in v2:
time: 102 us; the launch traced here: 101 us
  waiting for transfers between devices  48.8 us (48%)
  starting transfers between devices  39.9 us (39%)
  Pallas kernels  6.89 us (7%)
  local copies, waits for them, and re-layouts  3.66 us (4%)
  other arithmetic  1.07 us (1%)
  between operations  1.05 us (1%)
    ppermute x14, waiting for transfers between devices, send(): lax.ppermute(value, 'band', CORE_PAIRS if name == 'swap' else cube_pairs(...  26.9 us
    ppermute x12, starting transfers between devices, send(): return lax.ppermute(value, ('band', 'slab'), pairs)  21.9 us
    ppermute x12, waiting for transfers between devices, send(): return lax.ppermute(value, ('band', 'slab'), pairs)  20.4 us
    ppermute x14, starting transfers between devices, send(): lax.ppermute(value, 'band', CORE_PAIRS if name == 'swap' else cube_pairs(...  17.7 us
    pallas_call x1, Pallas kernels, step(): call(inverse_kernel, [SMEM] * 3 + [VMEM] * (3 + SENT + len(pieces)), (jax...  3.06 us
    pallas_call x1, Pallas kernels, step(): call(forward_kernel, [SMEM] * 2 + [VMEM] * (3 + len(pieces)), sent_shapes...  2.48 us
    squeeze x3, local copies, waits for them, and re-layouts, turn(): return lax.dynamic_index_in_dim(tables, slab, 0, keepdims=False)  2.32 us
  transfers between devices with their start and end apart: 28, of which 15 were waited for; matrix products, arithmetic and copies ran while one was open for 3% of the time, Pallas kernels for 0%

profile of v2, /device:TPU:64, one launch (start us, length us, event | category | flops | bytes accessed | tf_op | source)
XLA Modules:
  0.0 101.3 jit_solution(13432289644342262707)
XLA Ops:
  4.1 1.5 %collective-permute-start.1 = (f32[2,2,128,128]{3,2,1,0:T(8,128)S(1)}, f32[2,2,128,128]{3,2,1,0:T(8,128)S(1)}, u32[]{:S(2)}, u32[]{:S(2)}) collective-permute-start(f32[2,2,128,128]{3,2,1,0:T(8,128)S(1)} %get-tuple-element.33), channel_id=1, source_target_pairs={{0,16},{8,72},{16,0},{24,88},{32,48},{40,104},{48,32},{56,120},{64... | collective-permute-start | bytes 786440 | tf_op jit(solution)/shard_map/ppermute | solution.py:257
  5.6 2.1 %collective-permute-start.6 = (f32[2,2,128,128]{3,2,1,0:T(8,128)S(1)}, f32[2,2,128,128]{3,2,1,0:T(8,128)S(1)}, u32[]{:S(2)}, u32[]{:S(2)}) collective-permute-start(f32[2,2,128,128]{3,2,1,0:T(8,128)S(1)} %get-tuple-element.40), channel_id=1, source_target_pairs={{0,48},{8,200},{16,32},{24,216},{32,16},{40,232},{48,0},{56,248},{... | collective-permute-start | bytes 786440 | tf_op jit(solution)/shard_map/ppermute | solution.py:257
  7.8 5.3 %collective-permute-done.6 = f32[2,2,128,128]{3,2,1,0:T(8,128)S(1)} collective-permute-done((f32[2,2,128,128]{3,2,1,0:T(8,128)S(1)}, f32[2,2,128,128]{3,2,1,0:T(8,128)S(1)}, u32[]{:S(2)}, u32[]{:S(2)}) %collective-permute-start.6) | collective-permute-done | bytes 262176 | tf_op jit(solution)/shard_map/ppermute | solution.py:257
  13.3 1.7 %collective-permute-start.7 = (f32[2,2,128,128]{3,2,1,0:T(8,128)S(1)}, f32[2,2,128,128]{3,2,1,0:T(8,128)S(1)}, u32[]{:S(2)}, u32[]{:S(2)}) collective-permute-start(f32[2,2,128,128]{3,2,1,0:T(8,128)S(1)} %broadcast_select_fusion.4), channel_id=1, source_target_pairs={{0,64},{8,24},{16,80},{24,8},{32,96},{40,56},{48,112},{56,40},{64,... | collective-permute-start | bytes 786440 | tf_op jit(solution)/shard_map/ppermute | solution.py:257
  15.0 2.2 %collective-permute-start.3 = (f32[2,2,128,128]{3,2,1,0:T(8,128)S(1)}, f32[2,2,128,128]{3,2,1,0:T(8,128)S(1)}, u32[]{:S(2)}, u32[]{:S(2)}) collective-permute-start(f32[2,2,128,128]{3,2,1,0:T(8,128)S(1)} %broadcast_select_fusion.8), channel_id=1, source_target_pairs={{0,48},{8,200},{16,32},{24,216},{32,16},{40,232},{48,0},{56,248},{... | collective-permute-start | bytes 786440 | tf_op jit(solution)/shard_map/ppermute | solution.py:257
  17.2 2.5 %collective-permute-done.7 = f32[2,2,128,128]{3,2,1,0:T(8,128)S(1)} collective-permute-done((f32[2,2,128,128]{3,2,1,0:T(8,128)S(1)}, f32[2,2,128,128]{3,2,1,0:T(8,128)S(1)}, u32[]{:S(2)}, u32[]{:S(2)}) %collective-permute-start.7) | collective-permute-done | bytes 262176 | tf_op jit(solution)/shard_map/ppermute | solution.py:257
  19.8 3.1 %collective-permute-start.8 = (f32[2,2,128,128]{3,2,1,0:T(8,128)S(1)}, f32[2,2,128,128]{3,2,1,0:T(8,128)S(1)}, u32[]{:S(2)}, u32[]{:S(2)}) collective-permute-start(f32[2,2,128,128]{3,2,1,0:T(8,128)S(1)} %broadcast_select_fusion.5), channel_id=1, source_target_pairs={{0,192},{8,56},{16,208},{24,40},{32,224},{40,24},{48,240},{56,8},{... | collective-permute-start | bytes 786440 | tf_op jit(solution)/shard_map/ppermute | solution.py:257
  24.6 2.9 %collective-permute-done.8 = f32[2,2,128,128]{3,2,1,0:T(8,128)S(1)} collective-permute-done((f32[2,2,128,128]{3,2,1,0:T(8,128)S(1)}, f32[2,2,128,128]{3,2,1,0:T(8,128)S(1)}, u32[]{:S(2)}, u32[]{:S(2)}) %collective-permute-start.8) | collective-permute-done | bytes 262176 | tf_op jit(solution)/shard_map/ppermute | solution.py:257
  27.7 3.5 %collective-permute-done.4 = f32[2,2,128,128]{3,2,1,0:T(8,128)S(1)} collective-permute-done((f32[2,2,128,128]{3,2,1,0:T(8,128)S(1)}, f32[2,2,128,128]{3,2,1,0:T(8,128)S(1)}, u32[]{:S(2)}, u32[]{:S(2)}) %collective-permute-start.4) | collective-permute-done | bytes 262176 | tf_op jit(solution)/shard_map/ppermute | solution.py:257
  31.3 3.9 %collective-permute-start.5 = (f32[2,2,128,128]{3,2,1,0:T(8,128)S(1)}, f32[2,2,128,128]{3,2,1,0:T(8,128)S(1)}, u32[]{:S(2)}, u32[]{:S(2)}) collective-permute-start(f32[2,2,128,128]{3,2,1,0:T(8,128)S(1)} %broadcast_select_fusion.10), channel_id=1, source_target_pairs={{0,192},{8,56},{16,208},{24,40},{32,224},{40,24},{48,240},{56,8},{... | collective-permute-start | bytes 786440 | tf_op jit(solution)/shard_map/ppermute | solution.py:257
  36.3 6.0 %collective-permute-done.5 = f32[2,2,128,128]{3,2,1,0:T(8,128)S(1)} collective-permute-done((f32[2,2,128,128]{3,2,1,0:T(8,128)S(1)}, f32[2,2,128,128]{3,2,1,0:T(8,128)S(1)}, u32[]{:S(2)}, u32[]{:S(2)}) %collective-permute-start.5) | collective-permute-done | bytes 262176 | tf_op jit(solution)/shard_map/ppermute | solution.py:257
  43.2 5.7 %collective-permute-done.12.refs_4_.refs_11_ = f32[2,2,128,128]{3,2,1,0:T(8,128)S(1)} collective-permute-done((f32[2,2,128,128]{3,2,1,0:T(8,128)S(1)}, f32[2,2,128,128]{3,2,1,0:T(8,128)S(1)}, u32[]{:S(2)}, u32[]{:S(2)}) %collective-permute-start.12) | collective-permute-done | bytes 262176 | tf_op jit(solution)/shard_map/ppermute | solution.py:257
  50.4 2.5 %shard_map.104 = (f32[16,8,128]{2,1,0:T(8,128)S(1)}, f32[2,16,8,128]{3,2,1,0:T(8,128)S(1)}, f32[16,8,128]{2,1,0:T(8,128)S(1)}, f32[16,8,128]{2,1,0:T(8,128)S(1)}...) custom-call(s32[8]{0:T(128)S(1)} %stack.57.place_ref, s32[1]{0:T(128)} %bitcast.9.core_ref, ...), custom_call_target="tpu_custom_call" | custom-call | tf_op jit(solution)/shard_map/pallas_call | solution.py:346
  53.1 4.9 %collective-permute-done.19.refs_6_ = f32[2,16,8,128]{3,2,1,0:T(8,128)S(1)} collective-permute-done((f32[2,16,8,128]{3,2,1,0:T(8,128)S(1)}, f32[2,16,8,128]{3,2,1,0:T(8,128)S(1)}, u32[]{:S(2)}, u32[]{:S(2)}) %collective-permute-start.19) | collective-permute-done | bytes 131104 | tf_op jit(solution)/shard_map/ppermute | solution.py:314
  58.0 6.4 %collective-permute-start.20 = (f32[2,16,8,128]{3,2,1,0:T(8,128)S(1)}, f32[2,16,8,128]{3,2,1,0:T(8,128)S(1)}, u32[]{:S(2)}, u32[]{:S(2)}) collective-permute-start(f32[2,16,8,128]{3,2,1,0:T(8,128)S(1)} %pad_maximum_fusion.3), channel_id=1, source_target_pairs={{0,5},{1,6},{2,7},{3,0},{4,1},{5,2},{6,3},{7,4},{8,11},{9,12},{10,... | collective-permute-start | bytes 393224 | tf_op jit(solution)/shard_map/ppermute | solution.py:314
  64.4 4.4 %collective-permute-start.18 = (f32[16,8,128]{2,1,0:T(8,128)S(1)}, f32[16,8,128]{2,1,0:T(8,128)S(1)}, u32[]{:S(2)}, u32[]{:S(2)}) collective-permute-start(f32[16,8,128]{2,1,0:T(8,128)S(1)} %get-tuple-element.45), channel_id=1, source_target_pairs={{0,3},{1,4},{2,5},{3,6},{4,7},{5,0},{6,1},{7,2},{8,13},{9,14},{10,... | collective-permute-start | bytes 196616 | tf_op jit(solution)/shard_map/ppermute | solution.py:314
  70.1 5.0 %collective-permute-done.18.refs_3_ = f32[16,8,128]{2,1,0:T(8,128)S(1)} collective-permute-done((f32[16,8,128]{2,1,0:T(8,128)S(1)}, f32[16,8,128]{2,1,0:T(8,128)S(1)}, u32[]{:S(2)}, u32[]{:S(2)}) %collective-permute-start.18) | collective-permute-done | bytes 65568 | tf_op jit(solution)/shard_map/ppermute | solution.py:314
  77.9 4.4 %collective-permute-done.25.refs_6_ = f32[2,17,8,128]{3,2,1,0:T(8,128)S(1)} collective-permute-done((f32[2,17,8,128]{3,2,1,0:T(8,128)S(1)}, f32[2,17,8,128]{3,2,1,0:T(8,128)S(1)}, u32[]{:S(2)}, u32[]{:S(2)}) %collective-permute-start.25) | collective-permute-done | bytes 139296 | tf_op jit(solution)/shard_map/ppermute | solution.py:314
  82.4 3.6 %collective-permute-start.26 = (f32[2,17,8,128]{3,2,1,0:T(8,128)S(1)}, f32[2,17,8,128]{3,2,1,0:T(8,128)S(1)}, u32[]{:S(2)}, u32[]{:S(2)}) collective-permute-start(f32[2,17,8,128]{3,2,1,0:T(8,128)S(1)} %pad_maximum_fusion.2), channel_id=1, source_target_pairs={{0,5},{1,6},{2,7},{3,0},{4,1},{5,2},{6,3},{7,4},{8,11},{9,12},{10,... | collective-permute-start | bytes 417800 | tf_op jit(solution)/shard_map/ppermute | solution.py:314
  85.9 2.1 %collective-permute-start.23 = (f32[17,8,128]{2,1,0:T(8,128)S(1)}, f32[17,8,128]{2,1,0:T(8,128)S(1)}, u32[]{:S(2)}, u32[]{:S(2)}) collective-permute-start(f32[17,8,128]{2,1,0:T(8,128)S(1)} %get-tuple-element.51), channel_id=1, source_target_pairs={{0,2},{1,3},{2,4},{3,5},{4,6},{5,7},{6,0},{7,1},{8,14},{9,15},{10,... | collective-permute-start | bytes 208904 | tf_op jit(solution)/shard_map/ppermute | solution.py:314
  88.0 2.5 %collective-permute-start.24 = (f32[17,8,128]{2,1,0:T(8,128)S(1)}, f32[17,8,128]{2,1,0:T(8,128)S(1)}, u32[]{:S(2)}, u32[]{:S(2)}) collective-permute-start(f32[17,8,128]{2,1,0:T(8,128)S(1)} %get-tuple-element.52), channel_id=1, source_target_pairs={{0,3},{1,4},{2,5},{3,6},{4,7},{5,0},{6,1},{7,2},{8,13},{9,14},{10,... | collective-permute-start | bytes 208904 | tf_op jit(solution)/shard_map/ppermute | solution.py:314
  90.5 1.6 %collective-permute-start.27 = (f32[17,8,128]{2,1,0:T(8,128)S(1)}, f32[17,8,128]{2,1,0:T(8,128)S(1)}, u32[]{:S(2)}, u32[]{:S(2)}) collective-permute-start(f32[17,8,128]{2,1,0:T(8,128)S(1)} %get-tuple-element.55), channel_id=1, source_target_pairs={{0,6},{1,7},{2,0},{3,1},{4,2},{5,3},{6,4},{7,5},{8,10},{9,11},{10,... | collective-permute-start | bytes 208904 | tf_op jit(solution)/shard_map/ppermute | solution.py:314
  92.9 4.0 %collective-permute-done.24.refs_3_ = f32[17,8,128]{2,1,0:T(8,128)S(1)} collective-permute-done((f32[17,8,128]{2,1,0:T(8,128)S(1)}, f32[17,8,128]{2,1,0:T(8,128)S(1)}, u32[]{:S(2)}, u32[]{:S(2)}) %collective-permute-start.24) | collective-permute-done | bytes 69664 | tf_op jit(solution)/shard_map/ppermute | solution.py:314
  98.3 3.1 %shard_map.106 = (f32[1,16,128,128]{3,2,1,0:T(8,128)}, f32[1,768]{1,0:T(1,128)}) custom-call(s32[8]{0:T(128)S(1)} %stack.57.place_ref, s32[1]{0:T(128)} %bitcast.8.slab_ref, s32[1]{0:T(128)} %bitcast.9.core_ref, s32[1,768]{1,0:T(1,128)S(1)} %copy-done.3, bf16[128,128]{1,0:T(8,128)(2,1)S(1)} %dynamic-slice_bitcast_fusion.7.ty_ref, ...), custom_call_target="tpu_custom_call" | custom-call | tf_op jit(solution)/shard_map/pallas_call | solution.py:355
  (71 shorter events, 15.6 us)
Async XLA Ops:
  4.1 10.9 %collective-permute-start.1 = (f32[2,2,128,128]{3,2,1,0:T(8,128)S(1)}, f32[2,2,128,128]{3,2,1,0:T(8,128)S(1)}, u32[]{:S(2)}, u32[]{:S(2)}) collective-permute-start(f32[2,2,128,128]{3,2,1,0:T(8,128)S(1)} %get-tuple-element.33), channel_id=1, source_target_pairs={{0,16},{8,72},{16,0},{24,88},{32,48},{40,104},{48,32},{56,120},{64... | collective-permute-start | bytes 786440 | tf_op jit(solution)/shard_map/ppermute | solution.py:257
  5.6 7.6 %collective-permute-start.6 = (f32[2,2,128,128]{3,2,1,0:T(8,128)S(1)}, f32[2,2,128,128]{3,2,1,0:T(8,128)S(1)}, u32[]{:S(2)}, u32[]{:S(2)}) collective-permute-start(f32[2,2,128,128]{3,2,1,0:T(8,128)S(1)} %get-tuple-element.40), channel_id=1, source_target_pairs={{0,48},{8,200},{16,32},{24,216},{32,16},{40,232},{48,0},{56,248},{... | collective-permute-start | bytes 786440 | tf_op jit(solution)/shard_map/ppermute | solution.py:257
  13.3 6.5 %collective-permute-start.7 = (f32[2,2,128,128]{3,2,1,0:T(8,128)S(1)}, f32[2,2,128,128]{3,2,1,0:T(8,128)S(1)}, u32[]{:S(2)}, u32[]{:S(2)}) collective-permute-start(f32[2,2,128,128]{3,2,1,0:T(8,128)S(1)} %broadcast_select_fusion.4), channel_id=1, source_target_pairs={{0,64},{8,24},{16,80},{24,8},{32,96},{40,56},{48,112},{56,40},{64,... | collective-permute-start | bytes 786440 | tf_op jit(solution)/shard_map/ppermute | solution.py:257
  15.0 8.2 %collective-permute-start.3 = (f32[2,2,128,128]{3,2,1,0:T(8,128)S(1)}, f32[2,2,128,128]{3,2,1,0:T(8,128)S(1)}, u32[]{:S(2)}, u32[]{:S(2)}) collective-permute-start(f32[2,2,128,128]{3,2,1,0:T(8,128)S(1)} %broadcast_select_fusion.8), channel_id=1, source_target_pairs={{0,48},{8,200},{16,32},{24,216},{32,16},{40,232},{48,0},{56,248},{... | collective-permute-start | bytes 786440 | tf_op jit(solution)/shard_map/ppermute | solution.py:257
  19.8 7.7 %collective-permute-start.8 = (f32[2,2,128,128]{3,2,1,0:T(8,128)S(1)}, f32[2,2,128,128]{3,2,1,0:T(8,128)S(1)}, u32[]{:S(2)}, u32[]{:S(2)}) collective-permute-start(f32[2,2,128,128]{3,2,1,0:T(8,128)S(1)} %broadcast_select_fusion.5), channel_id=1, source_target_pairs={{0,192},{8,56},{16,208},{24,40},{32,224},{40,24},{48,240},{56,8},{... | collective-permute-start | bytes 786440 | tf_op jit(solution)/shard_map/ppermute | solution.py:257
  23.3 7.9 %collective-permute-start.4 = (f32[2,2,128,128]{3,2,1,0:T(8,128)S(1)}, f32[2,2,128,128]{3,2,1,0:T(8,128)S(1)}, u32[]{:S(2)}, u32[]{:S(2)}) collective-permute-start(f32[2,2,128,128]{3,2,1,0:T(8,128)S(1)} %broadcast_select_fusion.9), channel_id=1, source_target_pairs={{0,64},{8,24},{16,80},{24,8},{32,96},{40,56},{48,112},{56,40},{64,... | collective-permute-start | bytes 786440 | tf_op jit(solution)/shard_map/ppermute | solution.py:257
  27.6 7.6 %collective-permute-start.9 = (f32[2,2,128,128]{3,2,1,0:T(8,128)S(1)}, f32[2,2,128,128]{3,2,1,0:T(8,128)S(1)}, u32[]{:S(2)}, u32[]{:S(2)}) collective-permute-start(f32[2,2,128,128]{3,2,1,0:T(8,128)S(1)} %broadcast_select_fusion.6), channel_id=1, source_target_pairs={{0,16},{8,72},{16,0},{24,88},{32,48},{40,104},{48,32},{56,120},{64... | collective-permute-start | bytes 786440 | tf_op jit(solution)/shard_map/ppermute | solution.py:257
  31.3 11.0 %collective-permute-start.5 = (f32[2,2,128,128]{3,2,1,0:T(8,128)S(1)}, f32[2,2,128,128]{3,2,1,0:T(8,128)S(1)}, u32[]{:S(2)}, u32[]{:S(2)}) collective-permute-start(f32[2,2,128,128]{3,2,1,0:T(8,128)S(1)} %broadcast_select_fusion.10), channel_id=1, source_target_pairs={{0,192},{8,56},{16,208},{24,40},{32,224},{40,24},{48,240},{56,8},{... | collective-permute-start | bytes 786440 | tf_op jit(solution)/shard_map/ppermute | solution.py:257
  35.3 7.8 %collective-permute-start.13 = (f32[2,2,128,128]{3,2,1,0:T(8,128)S(1)}, f32[2,2,128,128]{3,2,1,0:T(8,128)S(1)}, u32[]{:S(2)}, u32[]{:S(2)}) collective-permute-start(f32[2,2,128,128]{3,2,1,0:T(8,128)S(1)} %broadcast_select_fusion.7.refs_1_.refs_8_), channel_id=1, source_target_pairs={{0,48},{8,200},{16,32},{24,216},{32,16},{40,232},{48,0},{56,248},{... | collective-permute-start | bytes 786440 | tf_op jit(solution)/shard_map/ppermute | solution.py:257
  42.4 6.5 %collective-permute-start.12 = (f32[2,2,128,128]{3,2,1,0:T(8,128)S(1)}, f32[2,2,128,128]{3,2,1,0:T(8,128)S(1)}, u32[]{:S(2)}, u32[]{:S(2)}) collective-permute-start(f32[2,2,128,128]{3,2,1,0:T(8,128)S(1)} %broadcast_select_fusion.11.refs_0_.refs_7_), channel_id=1, source_target_pairs={{0,16},{8,72},{16,0},{24,88},{32,48},{40,104},{48,32},{56,120},{64... | collective-permute-start | bytes 786440 | tf_op jit(solution)/shard_map/ppermute | solution.py:257
  42.5 7.2 %collective-permute-start.11 = (f32[2,2,128,128]{3,2,1,0:T(8,128)S(1)}, f32[2,2,128,128]{3,2,1,0:T(8,128)S(1)}, u32[]{:S(2)}, u32[]{:S(2)}) collective-permute-start(f32[2,2,128,128]{3,2,1,0:T(8,128)S(1)} %broadcast_select_fusion.7.refs_1_.refs_8_), channel_id=1, source_target_pairs={{0,8},{8,0},{16,24},{24,16},{32,40},{40,32},{48,56},{56,48},{64,72... | collective-permute-start | bytes 786440 | tf_op jit(solution)/shard_map/ppermute | solution.py:257
  42.6 7.1 %collective-permute-start.10 = (f32[2,2,128,128]{3,2,1,0:T(8,128)S(1)}, f32[2,2,128,128]{3,2,1,0:T(8,128)S(1)}, u32[]{:S(2)}, u32[]{:S(2)}) collective-permute-start(f32[2,2,128,128]{3,2,1,0:T(8,128)S(1)} %broadcast_select_fusion.11.refs_0_.refs_7_), channel_id=1, source_target_pairs={{0,8},{8,0},{16,24},{24,16},{32,40},{40,32},{48,56},{56,48},{64,72... | collective-permute-start | bytes 786440 | tf_op jit(solution)/shard_map/ppermute | solution.py:257
  43.1 6.6 %collective-permute-start.15 = (f32[2,2,128,128]{3,2,1,0:T(8,128)S(1)}, f32[2,2,128,128]{3,2,1,0:T(8,128)S(1)}, u32[]{:S(2)}, u32[]{:S(2)}) collective-permute-start(f32[2,2,128,128]{3,2,1,0:T(8,128)S(1)} %collective-permute-done.13.refs_5_.refs_12_), channel_id=1, source_target_pairs={{0,8},{8,0},{16,24},{24,16},{32,40},{40,32},{48,56},{56,48},{64,72... | collective-permute-start | bytes 786440 | tf_op jit(solution)/shard_map/ppermute | solution.py:257
  58.0 17.9 %collective-permute-start.20 = (f32[2,16,8,128]{3,2,1,0:T(8,128)S(1)}, f32[2,16,8,128]{3,2,1,0:T(8,128)S(1)}, u32[]{:S(2)}, u32[]{:S(2)}) collective-permute-start(f32[2,16,8,128]{3,2,1,0:T(8,128)S(1)} %pad_maximum_fusion.3), channel_id=1, source_target_pairs={{0,5},{1,6},{2,7},{3,0},{4,1},{5,2},{6,3},{7,4},{8,11},{9,12},{10,... | collective-permute-start | bytes 393224 | tf_op jit(solution)/shard_map/ppermute | solution.py:314
  64.4 5.7 %collective-permute-start.16 = (f32[16,8,128]{2,1,0:T(8,128)S(1)}, f32[16,8,128]{2,1,0:T(8,128)S(1)}, u32[]{:S(2)}, u32[]{:S(2)}) collective-permute-start(f32[16,8,128]{2,1,0:T(8,128)S(1)} %get-tuple-element.43), channel_id=1, source_target_pairs={{0,1},{1,2},{2,3},{3,4},{4,5},{5,6},{6,7},{7,0},{8,15},{9,8},{10,9... | collective-permute-start | bytes 196616 | tf_op jit(solution)/shard_map/ppermute | solution.py:314
  64.4 5.7 %collective-permute-start.17 = (f32[16,8,128]{2,1,0:T(8,128)S(1)}, f32[16,8,128]{2,1,0:T(8,128)S(1)}, u32[]{:S(2)}, u32[]{:S(2)}) collective-permute-start(f32[16,8,128]{2,1,0:T(8,128)S(1)} %get-tuple-element.44), channel_id=1, source_target_pairs={{0,2},{1,3},{2,4},{3,5},{4,6},{5,7},{6,0},{7,1},{8,14},{9,15},{10,... | collective-permute-start | bytes 196616 | tf_op jit(solution)/shard_map/ppermute | solution.py:314
  64.4 10.7 %collective-permute-start.18 = (f32[16,8,128]{2,1,0:T(8,128)S(1)}, f32[16,8,128]{2,1,0:T(8,128)S(1)}, u32[]{:S(2)}, u32[]{:S(2)}) collective-permute-start(f32[16,8,128]{2,1,0:T(8,128)S(1)} %get-tuple-element.45), channel_id=1, source_target_pairs={{0,3},{1,4},{2,5},{3,6},{4,7},{5,0},{6,1},{7,2},{8,13},{9,14},{10,... | collective-permute-start | bytes 196616 | tf_op jit(solution)/shard_map/ppermute | solution.py:314
  68.8 7.1 %collective-permute-start.21 = (f32[16,8,128]{2,1,0:T(8,128)S(1)}, f32[16,8,128]{2,1,0:T(8,128)S(1)}, u32[]{:S(2)}, u32[]{:S(2)}) collective-permute-start(f32[16,8,128]{2,1,0:T(8,128)S(1)} %get-tuple-element.48), channel_id=1, source_target_pairs={{0,6},{1,7},{2,0},{3,1},{4,2},{5,3},{6,4},{7,5},{8,10},{9,11},{10,... | collective-permute-start | bytes 196616 | tf_op jit(solution)/shard_map/ppermute | solution.py:314
  77.2 5.1 %collective-permute-start.25 = (f32[2,17,8,128]{3,2,1,0:T(8,128)S(1)}, f32[2,17,8,128]{3,2,1,0:T(8,128)S(1)}, u32[]{:S(2)}, u32[]{:S(2)}) collective-permute-start(f32[2,17,8,128]{3,2,1,0:T(8,128)S(1)} %get-tuple-element.54), channel_id=1, source_target_pairs={{0,7},{1,0},{2,1},{3,2},{4,3},{5,4},{6,5},{7,6},{8,9},{9,10},{10,1... | collective-permute-start | bytes 417800 | tf_op jit(solution)/shard_map/ppermute | solution.py:314
  82.4 15.9 %collective-permute-start.26 = (f32[2,17,8,128]{3,2,1,0:T(8,128)S(1)}, f32[2,17,8,128]{3,2,1,0:T(8,128)S(1)}, u32[]{:S(2)}, u32[]{:S(2)}) collective-permute-start(f32[2,17,8,128]{3,2,1,0:T(8,128)S(1)} %pad_maximum_fusion.2), channel_id=1, source_target_pairs={{0,5},{1,6},{2,7},{3,0},{4,1},{5,2},{6,3},{7,4},{8,11},{9,12},{10,... | collective-permute-start | bytes 417800 | tf_op jit(solution)/shard_map/ppermute | solution.py:314
  85.9 7.0 %collective-permute-start.22 = (f32[17,8,128]{2,1,0:T(8,128)S(1)}, f32[17,8,128]{2,1,0:T(8,128)S(1)}, u32[]{:S(2)}, u32[]{:S(2)}) collective-permute-start(f32[17,8,128]{2,1,0:T(8,128)S(1)} %get-tuple-element.50), channel_id=1, source_target_pairs={{0,1},{1,2},{2,3},{3,4},{4,5},{5,6},{6,7},{7,0},{8,15},{9,8},{10,9... | collective-permute-start | bytes 208904 | tf_op jit(solution)/shard_map/ppermute | solution.py:314
  85.9 7.0 %collective-permute-start.23 = (f32[17,8,128]{2,1,0:T(8,128)S(1)}, f32[17,8,128]{2,1,0:T(8,128)S(1)}, u32[]{:S(2)}, u32[]{:S(2)}) collective-permute-start(f32[17,8,128]{2,1,0:T(8,128)S(1)} %get-tuple-element.51), channel_id=1, source_target_pairs={{0,2},{1,3},{2,4},{3,5},{4,6},{5,7},{6,0},{7,1},{8,14},{9,15},{10,... | collective-permute-start | bytes 208904 | tf_op jit(solution)/shard_map/ppermute | solution.py:314
  88.0 8.8 %collective-permute-start.24 = (f32[17,8,128]{2,1,0:T(8,128)S(1)}, f32[17,8,128]{2,1,0:T(8,128)S(1)}, u32[]{:S(2)}, u32[]{:S(2)}) collective-permute-start(f32[17,8,128]{2,1,0:T(8,128)S(1)} %get-tuple-element.52), channel_id=1, source_target_pairs={{0,3},{1,4},{2,5},{3,6},{4,7},{5,0},{6,1},{7,2},{8,13},{9,14},{10,... | collective-permute-start | bytes 208904 | tf_op jit(solution)/shard_map/ppermute | solution.py:314
  90.5 7.7 %collective-permute-start.27 = (f32[17,8,128]{2,1,0:T(8,128)S(1)}, f32[17,8,128]{2,1,0:T(8,128)S(1)}, u32[]{:S(2)}, u32[]{:S(2)}) collective-permute-start(f32[17,8,128]{2,1,0:T(8,128)S(1)} %get-tuple-element.55), channel_id=1, source_target_pairs={{0,6},{1,7},{2,0},{3,1},{4,2},{5,3},{6,4},{7,5},{8,10},{9,11},{10,... | collective-permute-start | bytes 208904 | tf_op jit(solution)/shard_map/ppermute | solution.py:314
  (9 other events, 45.4 us)
